TPU v7x, 128 devices: a whole 4x4x4 slice. The times are simulated.
128 devices in a mesh: row: 16 (over z, x), col: 8 (over y, core).
Axes of the slice: x: 4, y: 4, z: 4, core: 2. Of those that a mesh axis runs over, the one named last changes fastest.
Arguments:
- features: bfloat16 [65536, 256], P(('col', 'row')), may hold values from -6 to 6
- adjacency: bfloat16 [512, 8, 12, 128, 128], P('row', 'col'), may hold values from 0 to 0.023925781
- block_cols: int32 [512, 8, 12], P('row', 'col'), may hold values from 0 to 63, as said below
- block_live: int32 [512, 8], P('row', 'col'), may hold values from 1 to 12, as said below
- weight: bfloat16 [256, 256], replicated, may hold values from -0.375 to 0.375
- bias: float32 [256], replicated, may hold values from -3 to 3
- upstream: bfloat16 [65536, 256], P(('row', 'col')), may hold values from -6 to 6
Outputs:
- activations: bfloat16 [65536, 256], P(('row', 'col'))
- feature_grad: bfloat16 [65536, 256], P(('col', 'row'))
- weight_grad: float32 [256, 256], replicated
- bias_grad: float32 [256], replicated
Inputs may be any that keep to these rules, and one draw needn't show every extreme that they name: `block_cols`: the live slots of one block row in one column tile name distinct column blocks of that tile. Slots k with k < block_live[i, c] are live; the other slots of block_cols and adjacency are ignored. Some entry equals 12.
All inputs are finite; a program needn't handle non-finite values.
Results may differ from a plain program's by a relative error of at most 0.014.
Values may be sent and summed in bfloat16 or wider, within the bound.
A program may use at most 256 MiB of HBM per device.

v0:
```python
import jax
import jax.numpy as jnp
from jax import lax
from jax.sharding import PartitionSpec as P


def local(features, adjacency, block_cols, block_live, weight, bias, upstream):
    block_rows = adjacency.shape[0]
    block_slots = adjacency.shape[2]
    block_size = adjacency.shape[3]
    feature_width = features.shape[1]
    tile_blocks = adjacency.reshape(block_rows, block_slots, block_size, block_size)
    column_ids = block_cols.reshape(block_rows, block_slots)
    live_count = block_live.reshape(block_rows)
    live_mask = lax.broadcasted_iota(jnp.int32, (block_rows, block_slots), 1) < live_count[:, None]
    feature_panel = lax.all_gather(features, "row", axis=0, tiled=True)
    panel_blocks = feature_panel.shape[0] // block_size
    picked = feature_panel.reshape(panel_blocks, block_size, feature_width)[column_ids]
    picked = jnp.where(live_mask[:, :, None, None], picked, jnp.zeros((), jnp.bfloat16))
    partial_value = jnp.einsum(
        "ikab,ikbf->iaf", tile_blocks, picked, preferred_element_type=jnp.float32
    )
    partial_value = partial_value.reshape(block_rows * block_size, feature_width)
    aggregated = lax.psum_scatter(partial_value, "col", scatter_dimension=0, tiled=True).astype(
        jnp.bfloat16
    )
    preact = jnp.dot(aggregated, weight, preferred_element_type=jnp.float32) + bias
    sigmoid_pre = jax.nn.sigmoid(preact)
    outputs_here = (preact * sigmoid_pre).astype(jnp.bfloat16)
    derivative = sigmoid_pre * (1.0 + preact * (1.0 - sigmoid_pre))
    grad_pre = (upstream.astype(jnp.float32) * derivative).astype(jnp.bfloat16)
    weight_part = jnp.einsum("nf,ng->fg", aggregated, grad_pre, preferred_element_type=jnp.float32)
    bias_part = jnp.sum(grad_pre.astype(jnp.float32), axis=0)
    grad_agg = jnp.einsum("ng,fg->nf", grad_pre, weight, preferred_element_type=jnp.float32).astype(
        jnp.bfloat16
    )
    weight_grad, bias_grad = lax.psum((weight_part, bias_part), ("row", "col"))
    tile_grad = lax.all_gather(grad_agg, "col", axis=0, tiled=True)
    contrib = jnp.einsum(
        "ikab,iaf->ikbf",
        tile_blocks,
        tile_grad.reshape(block_rows, block_size, feature_width),
        preferred_element_type=jnp.float32,
    )
    contrib = contrib.reshape(block_rows * block_slots, block_size, feature_width)
    target_blocks = jnp.where(live_mask, column_ids, panel_blocks).reshape(-1)
    panel_sum = jnp.zeros((panel_blocks, block_size, feature_width), jnp.float32)
    panel_sum = panel_sum.at[target_blocks].add(contrib, mode="drop")
    panel_sum = panel_sum.reshape(panel_blocks * block_size, feature_width)
    feature_grad = lax.psum_scatter(
        panel_sum.astype(jnp.bfloat16), "row", scatter_dimension=0, tiled=True
    )
    return (outputs_here, feature_grad, weight_grad, bias_grad)


def solution(mesh):
    placed = (
        P(("col", "row"), None),
        P("row", "col", None, None, None),
        P("row", "col", None),
        P("row", "col"),
        P(),
        P(),
        P(("row", "col"), None),
    )
    return jax.shard_map(
        local,
        mesh=mesh,
        in_specs=placed,
        out_specs=(P(("row", "col"), None), P(("col", "row"), None), P(), P()),
        check_vma=False,
    )
```

profile of v0, /device:TPU:1, one launch (start us, length us, event | category | flops | bytes accessed | tf_op | source)
XLA Modules:
  0.0 439.4 jit_solution(6922542560461976531)
XLA Ops:
  7.2 0.7 all-gather.3.cloned.1.call-update
  8.0 0.7 compare_select_fusion
  8.7 0.1 copy.12
  8.8 0.1 reshape.129
  8.9 0.7 iota_compare_fusion
  9.6 55.5 %all-gather.3.cloned.1.call-done = bf16[8192,256]{1,0:T(8,128)(2,1)} async-done(((bf16[512,256]{1,0:T(8,128)(2,1)}), bf16[8192,256]{1,0:T(8,128)(2,1)}) %all-gather.3.cloned.1.call-update) | async-done | bytes 4194320 | tf_op jit(solution)/shard_map/all_gather | solution.py:16
  65.1 15.1 %gather_fusion = bf16[384,128,256]{2,1,0:T(8,128)(2,1)} fusion(bf16[64,128,256]{2,1,0:T(8,128)(2,1)} %bitcast.35, s32[1024]{0:T(1024)S(1)} %pad_clamp_fusion), kind=kCustom, calls=%fused_computation | custom fusion | bytes 50333184 | tf_op jit(solution)/shard_map/gather | solution.py:18
  80.2 16.1 %fusion = f32[32,256,128,1]{1,2,3,0:T(8,128)} fusion(bf16[32,12,128,256]{3,2,1,0:T(8,128)(2,1)} %bitcast.36, pred[32,12]{1,0:T(8,128)(4,1)S(1)} %iota_compare_fusion, bf16[32,1,12,128,128]{4,3,2,1,0:T(8,128)(2,1)} %param.8), kind=kOutput, calls=%fused_computation.2 | convolution fusion | flops 3233808384 | bytes 41943424 | tf_op jit(solution)/shard_map/ikab,ikbf->iaf/dot_general | solution.py:20
  96.3 34.5 %reduce-scatter.3.cloned.1.call-done = f32[512,256]{1,0:T(8,128)} async-done(((f32[4096,256]{1,0:T(8,128)}), f32[512,256]{1,0:T(8,128)}) %reduce-scatter.3.cloned.1.call-update) | async-done | bytes 524304 | tf_op jit(solution)/shard_map/reduce_scatter | solution.py:24
  130.9 2.2 convert_reduce_fusion
  133.1 1.0 convolution_convert_fusion
  134.1 0.1 lt.53
  134.2 0.1 copy.13
  134.3 0.1 reshape.124
  134.4 2.0 fusion.7
  136.5 25.1 %all-gather.5.cloned.1.call-done = bf16[4096,256]{1,0:T(8,128)(2,1)} async-done(((bf16[512,256]{1,0:T(8,128)(2,1)}), bf16[4096,256]{1,0:T(8,128)(2,1)}) %all-gather.5.cloned.1.call-update) | async-done | bytes 2097168 | tf_op jit(solution)/shard_map/all_gather | solution.py:38
  161.7 22.5 %fusion.3 = f32[32,256,12,128]{3,1,2,0:T(8,128)} fusion(bf16[32,128,256,1]{2,1,3,0:T(8,128)(2,1)} %bitcast.39, bf16[32,1,12,128,128]{4,3,2,1,0:T(8,128)(2,1)} %param.8), kind=kOutput, calls=%fused_computation.5 | convolution fusion | flops 3221225472 | bytes 65011712 | tf_op jit(solution)/shard_map/ikab,iaf->ikbf/dot_general | solution.py:39
  184.1 48.8 %copy.15 = f32[384,128,256]{2,1,0:T(8,128)} copy(f32[384,128,256]{1,2,0:T(8,128)} %bitcast.34) | data formatting | bytes 100663296 | tf_op jit(solution)/shard_map/reshape | solution.py:45
  233.0 4.2 broadcast_in_dim.23
  237.2 111.1 %scatter_fusion = f32[64,128,256]{2,1,0:T(8,128)} fusion(f32[64,128,256]{2,1,0:T(8,128)} %broadcast_in_dim.23, s32[384]{0:T(512)S(1)} %fusion.10, f32[384,128,256]{2,1,0:T(8,128)} %copy.15), kind=kCustom, calls=%fused_computation.1 | custom fusion | flops 12582912 | bytes 150996480 | tf_op jit(solution)/shard_map/scatter-add | solution.py:48
  348.3 5.9 %convert_element_type.29 = bf16[64,128,256]{2,1,0:T(8,128)(2,1)} convert(f32[64,128,256]{2,1,0:T(8,128)} %scatter_fusion) | non-fusion elementwise | flops 2097152 | bytes 12582912 | tf_op jit(solution)/shard_map/convert_element_type | solution.py:51
  354.3 65.5 %psum.15 = f32[256]{0:T(256)} all-reduce(f32[256]{0:T(256)S(1)} %get-tuple-element.4), channel_id=1, replica_groups=mesh['row'=16,'col'=8] {'row','col'}, use_global_device_ids=true, to_apply=%region_5.6 | all-reduce | flops 256 | bytes 2048 | tf_op jit(solution)/shard_map/psum | solution.py:37
  419.7 11.5 %reduce-scatter.5.cloned.1.call-done = bf16[512,256]{1,0:T(8,128)(2,1)} async-done(((bf16[8192,256]{1,0:T(8,128)(2,1)}), bf16[512,256]{1,0:T(8,128)(2,1)}) %reduce-scatter.5.cloned.1.call-update) | async-done | bytes 262160 | tf_op jit(solution)/shard_map/reduce_scatter | solution.py:50
  431.2 1.7 copy.22
  (22 shorter events, 0.3 us)
Async XLA Ops:
  7.2 123.7 %copy-start = (bf16[256,256]{1,0:T(8,128)(2,1)S(1)}, bf16[256,256]{1,0:T(8,128)(2,1)}, u32[]{:S(2)}) copy-start(bf16[256,256]{1,0:T(8,128)(2,1)} %param.11) | copy-start | bytes 393220
  7.2 57.9 %all-gather.3.cloned.1.call-start = ((), (), s32[]{:S(2)}) async-start(), calls=%async_computation.2 | async-start | bytes 4456448 | tf_op jit(solution)/shard_map/all_gather | solution.py:16
  7.9 123.0 %reduce-scatter.3.cloned.1.call-start = ((), (), s32[]{:S(2)}) async-start(), calls=%async_computation.3 | async-start | bytes 4718592 | tf_op jit(solution)/shard_map/reduce_scatter | solution.py:24
  80.2 50.7 %copy-start.3 = (bf16[512,256]{1,0:T(8,128)(2,1)S(1)}, bf16[512,256]{1,0:T(8,128)(2,1)}, u32[]{:S(2)}) copy-start(bf16[512,256]{1,0:T(8,128)(2,1)} %param.13) | copy-start | bytes 786436
  80.2 50.7 %copy-start.4 = (f32[256]{0:T(256)S(1)}, f32[256]{0:T(256)}, u32[]{:S(2)}) copy-start(f32[256]{0:T(256)} %param.12) | copy-start | bytes 3076
  80.2 54.0 %copy-start.2 = (s32[32,1,12]{0,1,2:T(1,128)S(1)}, s32[32,1,12]{0,1,2:T(1,128)}, u32[]{:S(2)}) copy-start(s32[32,1,12]{0,1,2:T(1,128)} %param.9) | copy-start | bytes 4612
  96.3 65.4 %all-gather.5.cloned.1.call-start = ((), (), s32[]{:S(2)}) async-start(), calls=%async_computation.4 | async-start | bytes 2359296 | tf_op jit(solution)/shard_map/all_gather | solution.py:38
  134.0 285.7 %all-reduce.2.cloned.1.call-start = ((), (), s32[]{:S(2)}) async-start(), calls=%async_computation.6 | async-start | bytes 524288 | tf_op jit(solution)/shard_map/psum | solution.py:37
  136.5 294.7 %reduce-scatter.5.cloned.1.call-start = ((), (), s32[]{:S(2)}) async-start(), calls=%async_computation.5 | async-start | bytes 4456448 | tf_op jit(solution)/shard_map/reduce_scatter | solution.py:50
  237.2 195.6 %copy-start.1 = (bf16[256,256]{1,0:T(8,128)(2,1)S(1)}, bf16[256,256]{1,0:T(8,128)(2,1)}, u32[]{:S(2)}) copy-start(bf16[256,256]{1,0:T(8,128)(2,1)} %param.11) | copy-start | bytes 393220
Sparse Core Ops, SparseCore 0:
  10.2 54.8 all-gather.2
  96.4 34.4 reduce-scatter.2
  134.2 27.4 all-gather.4
  166.8 141.4 all-reduce.1
  354.4 76.7 reduce-scatter.4
where the time goes:
time: 441 us; the launch traced here: 439 us
  waiting for transfers between devices  127 us (29%)
  other arithmetic  118 us (27%)
  local copies, waits for them, and re-layouts  70.4 us (16%)
  blocking collectives  65.5 us (15%)
  matrix products  43.7 us (10%)
  between operations  13.8 us (3%)
    scatter-add x1, other arithmetic, local(): panel_sum = panel_sum.at[target_blocks].add(contrib, mode='drop')  111 us
    psum x1, blocking collectives, local(): weight_grad, bias_grad = lax.psum((weight_part, bias_part), ('row', 'col'))  65.5 us
    all_gather x1, waiting for transfers between devices, local(): feature_panel = lax.all_gather(features, 'row', axis=0, tiled=True)  55.5 us
    reshape x1, local copies, waits for them, and re-layouts, local(): contrib.reshape(block_rows * block_slots, block_size, feature_width)  48.8 us
    reduce_scatter x1, waiting for transfers between devices, local(): lax.psum_scatter(partial_value, 'col', scatter_dimension=0, tiled=True)  34.5 us
    all_gather x1, waiting for transfers between devices, local(): tile_grad = lax.all_gather(grad_agg, 'col', axis=0, tiled=True)  25.1 us
    dot_general x1, matrix products, local(): jnp.einsum('ikab,iaf->ikbf', tile_blocks, tile_grad.reshape(block_rows, b...  22.5 us
    dot_general x1, matrix products, local(): jnp.einsum('ikab,ikbf->iaf', tile_blocks, picked, preferred_element_type=...  16.1 us
  transfers between devices with their start and end apart: 5, of which 4 were waited for; matrix products, arithmetic and copies ran while one was open for 45% of the time, Pallas kernels for 0%

commit v1 on v0

v1 whole, which is shorter than its diff:
```python
import jax
import jax.numpy as jnp
from jax import lax
from jax.experimental import pallas as pl
from jax.experimental.pallas import tpu as pltpu
from jax.sharding import PartitionSpec as P


def forward_body(cols_ref, adj_ref, panel_ref, out_ref):
    i = pl.program_id(0)
    slots = adj_ref.shape[1]
    total = None
    for k in range(0, slots, 2):
        left = jnp.concatenate([adj_ref[0, k], adj_ref[0, k + 1]], axis=1)
        blocks = []
        for s in (k, k + 1):
            j = cols_ref[i * slots + s]
            block = panel_ref[jnp.minimum(j, panel_ref.shape[0] - 1)]
            blocks.append(jnp.where(j < panel_ref.shape[0], block, jnp.zeros_like(block)))
        right = jnp.concatenate(blocks, axis=0)
        part = jnp.dot(left, right, preferred_element_type=jnp.float32)
        total = part if total is None else total + part
    out_ref[0] = total.astype(out_ref.dtype)


def backward_body(cols_ref, adj_ref, grad_ref, out_ref, acc_ref):
    i = pl.program_id(0)
    slots = adj_ref.shape[1]
    size = adj_ref.shape[3]

    @pl.when(i == 0)
    def _():
        acc_ref[...] = jnp.zeros_like(acc_ref)

    turned = grad_ref[0].T
    for k in range(0, slots, 2):
        right = jnp.concatenate([adj_ref[0, k], adj_ref[0, k + 1]], axis=1)
        part = jnp.dot(turned, right, preferred_element_type=jnp.float32)
        for s in (0, 1):
            j = cols_ref[i * slots + k + s]
            acc_ref[j] += part[:, s * size : (s + 1) * size]

    @pl.when(i == pl.num_programs(0) - 1)
    def _():
        @pl.loop(0, out_ref.shape[0])
        def _(j):
            out_ref[j] = acc_ref[j].astype(out_ref.dtype)


def forward_product(cols, adj, panel):
    rows, slots, size, _ = adj.shape
    width = panel.shape[2]
    return pl.pallas_call(
        forward_body,
        out_shape=jax.ShapeDtypeStruct((rows, size, width), jnp.bfloat16),
        grid_spec=pltpu.PrefetchScalarGridSpec(
            num_scalar_prefetch=1,
            grid=(rows,),
            in_specs=[
                pl.BlockSpec((1, slots, size, size), lambda i, c: (i, 0, 0, 0)),
                pl.BlockSpec(panel.shape, lambda i, c: (0, 0, 0), pipeline_mode=pl.Buffered(1)),
            ],
            out_specs=pl.BlockSpec((1, size, width), lambda i, c: (i, 0, 0)),
        ),
        compiler_params=pltpu.CompilerParams(vmem_limit_bytes=48 << 20),
        name="forward_product",
    )(cols, adj, panel)


def backward_product(cols, adj, grad, blocks):
    rows, slots, size, _ = adj.shape
    width = grad.shape[2]
    return pl.pallas_call(
        backward_body,
        out_shape=jax.ShapeDtypeStruct((blocks, width, size), jnp.bfloat16),
        grid_spec=pltpu.PrefetchScalarGridSpec(
            num_scalar_prefetch=1,
            grid=(rows,),
            in_specs=[
                pl.BlockSpec((1, slots, size, size), lambda i, c: (i, 0, 0, 0)),
                pl.BlockSpec((1, size, width), lambda i, c: (i, 0, 0)),
            ],
            out_specs=pl.BlockSpec((blocks, width, size), lambda i, c: (0, 0, 0)),
            scratch_shapes=[pltpu.VMEM((blocks + 1, width, size), jnp.float32)],
        ),
        compiler_params=pltpu.CompilerParams(vmem_limit_bytes=48 << 20),
        name="backward_product",
    )(cols, adj, grad)


def local(features, adjacency, block_cols, block_live, weight, bias, upstream):
    rows, _, slots, size, _ = adjacency.shape
    width = features.shape[1]
    adj = adjacency.reshape(rows, slots, size, size)
    blocks = features.shape[0] * lax.axis_size("row") // size
    live = lax.broadcasted_iota(jnp.int32, (rows, slots), 1) < block_live.reshape(rows)[:, None]
    cols = jnp.where(live, block_cols.reshape(rows, slots), blocks).reshape(-1)
    panel = lax.all_gather(features, "row", axis=0, tiled=True).reshape(blocks, size, width)
    partial = forward_product(cols, adj, panel).reshape(rows * size, width)
    aggregated = lax.psum_scatter(partial, "col", scatter_dimension=0, tiled=True)
    preact = jnp.dot(aggregated, weight, preferred_element_type=jnp.float32) + bias
    s = jax.nn.sigmoid(preact)
    activations = (preact * s).astype(jnp.bfloat16)
    derivative = s * (1.0 + preact * (1.0 - s))
    grad_pre = (upstream.astype(jnp.float32) * derivative).astype(jnp.bfloat16)
    weight_part = jnp.einsum("nf,ng->fg", aggregated, grad_pre, preferred_element_type=jnp.float32)
    bias_part = jnp.sum(grad_pre.astype(jnp.float32), axis=0)
    grad_agg = jnp.einsum("ng,fg->nf", grad_pre, weight, preferred_element_type=jnp.float32).astype(
        jnp.bfloat16
    )
    weight_grad, bias_grad = lax.psum((weight_part, bias_part), ("row", "col"))
    grad = lax.all_gather(grad_agg, "col", axis=0, tiled=True).reshape(rows, size, width)
    turned = backward_product(cols, adj, grad, blocks)
    mine = lax.psum_scatter(turned, "row", scatter_dimension=0, tiled=True)
    feature_grad = mine.transpose(0, 2, 1).reshape(features.shape)
    return (activations, feature_grad, weight_grad, bias_grad)


def solution(mesh):
    placed = (
        P(("col", "row"), None),
        P("row", "col", None, None, None),
        P("row", "col", None),
        P("row", "col"),
        P(),
        P(),
        P(("row", "col"), None),
    )
    return jax.shard_map(
        local,
        mesh=mesh,
        in_specs=placed,
        out_specs=(P(("row", "col"), None), P(("col", "row"), None), P(), P()),
        check_vma=False,
    )
```

time: 441 us -> 414 us (0.939)
  waiting for transfers between devices: 127 us -> 269 us
  other arithmetic: 118 us -> 0.73 us
  local copies, waits for them, and re-layouts: 70.4 us -> 6.93 us
  Pallas kernels: 0 us -> 52 us
  matrix products: 43.7 us -> 4 us
    psum x1, waiting for transfers between devices: 0.01 us -> 147 us  [local(): weight_grad, bias_grad = lax.psum((weight_part, bias_part), ('row', 'col'))]
    scatter-add x1 -> x0, other arithmetic: 111 us -> none  [local(): panel_sum = panel_sum.at[target_blocks].add(contrib, mode='drop')]
    pallas_call x0 -> x2, Pallas kernels: none -> 52 us  [the longest x1 27.5 us: backward_product(): pl.pallas_call(backward_body, out_shape=jax.ShapeDtypeStruct((blocks, wid...]
    reshape x2 -> x1, local copies, waits for them, and re-layouts: 48.9 us -> 0.1 us  [local(): cols = jnp.where(live, block_cols.reshape(rows, slots), blocks).reshape(-1)]
    dot_general x2 -> x0, matrix products: 38.6 us -> none  [the longest x1 22.5 us: local(): jnp.einsum('ikab,iaf->ikbf', tile_blocks, tile_grad.reshape(block_rows, b...]
    gather x1 -> x0, local copies, waits for them, and re-layouts: 15.1 us -> none  [local(): feature_panel.reshape(panel_blocks, block_size, feature_width)[column_ids]]
    reduce_scatter x2, waiting for transfers between devices: 46 us -> 38.5 us  [the longest x1 30.4 us: local(): lax.psum_scatter(partial, 'col', scatter_dimension=0, tiled=True)]
    convert_element_type x1 -> x0, other arithmetic: 5.94 us -> none  [local(): panel_sum.astype(jnp.bfloat16)]
  transfers between devices with their start and end apart: 5 -> 5, of which waited for: 4 -> 5; matrix products, arithmetic and copies ran while one was open for 45% -> 1% of each run, Pallas kernels for 0% -> 0%
where the time goes in v1:
time: 414 us; the launch traced here: 413 us
  waiting for transfers between devices  269 us (65%)
  blocking collectives  66.2 us (16%)
  Pallas kernels  52 us (13%)
  between operations  13.8 us (3%)
  local copies, waits for them, and re-layouts  6.93 us (2%)
    psum x1, waiting for transfers between devices, local(): weight_grad, bias_grad = lax.psum((weight_part, bias_part), ('row', 'col'))  147 us
    psum x1, blocking collectives, local(): weight_grad, bias_grad = lax.psum((weight_part, bias_part), ('row', 'col'))  66.2 us
    all_gather x1, waiting for transfers between devices, local(): lax.all_gather(features, 'row', axis=0, tiled=True)  55.4 us
    reduce_scatter x1, waiting for transfers between devices, local(): lax.psum_scatter(partial, 'col', scatter_dimension=0, tiled=True)  30.4 us
    pallas_call x1, Pallas kernels, backward_product(): pl.pallas_call(backward_body, out_shape=jax.ShapeDtypeStruct((blocks, wid...  27.5 us
    all_gather x1, waiting for transfers between devices, local(): lax.all_gather(grad_agg, 'col', axis=0, tiled=True)  27.5 us
    pallas_call x1, Pallas kernels, forward_product(): pl.pallas_call(forward_body, out_shape=jax.ShapeDtypeStruct((rows, size,...  24.5 us
  transfers between devices with their start and end apart: 5, of which 5 were waited for; matrix products, arithmetic and copies ran while one was open for 1% of the time, Pallas kernels for 0%

profile of v1, /device:TPU:1, one launch (start us, length us, event | category | flops | bytes accessed | tf_op | source)
XLA Modules:
  0.0 412.6 jit_solution(9318575717327039977)
XLA Ops:
  7.2 0.7 all-gather.3.cloned.1.call-update
  7.9 0.0 reduce-scatter.3.cloned.1.call-start
  8.0 0.7 iota_compare_fusion
  8.7 0.1 lt.17
  8.8 0.8 copy.11
  9.6 0.1 reshape.32
  9.7 55.4 %all-gather.3.cloned.1.call-done = bf16[8192,256]{1,0:T(8,128)(2,1)} async-done(((bf16[512,256]{1,0:T(8,128)(2,1)}), bf16[8192,256]{1,0:T(8,128)(2,1)}) %all-gather.3.cloned.1.call-update) | async-done | bytes 4194320 | tf_op jit(solution)/shard_map/all_gather | solution.py:98
  65.1 24.5 %forward_product.1 = bf16[32,128,256]{2,1,0:T(8,128)(2,1)} custom-call(s32[384]{0:T(512)S(1)} %broadcast_select_fusion.cols_ref, bf16[32,12,128,128]{3,2,1,0:T(8,128)(2,1)} %bitcast.16, bf16[64,128,256]{2,1,0:T(8,128)(2,1)} %bitcast.18), custom_call_target="tpu_custom_call" | custom-call | tf_op jit(solution)/shard_map/forward_product/pallas_call | solution.py:53
  89.6 0.0 all-gather.5.cloned.1.call-start
  89.6 30.4 %reduce-scatter.3.cloned.1.call-done = bf16[512,256]{1,0:T(8,128)(2,1)} async-done(((bf16[4096,256]{1,0:T(8,128)(2,1)}), bf16[512,256]{1,0:T(8,128)(2,1)}) %reduce-scatter.3.cloned.1.call-update) | async-done | bytes 262160 | tf_op jit(solution)/shard_map/reduce_scatter | solution.py:100
  120.0 2.1 convert_reduce_fusion
  122.1 1.0 convolution_convert_fusion
  123.0 0.0 reduce-scatter.5.cloned.1.call-start
  123.1 27.5 %all-gather.5.cloned.1.call-done = bf16[4096,256]{1,0:T(8,128)(2,1)} async-done(((bf16[512,256]{1,0:T(8,128)(2,1)}), bf16[4096,256]{1,0:T(8,128)(2,1)}) %all-gather.5.cloned.1.call-update) | async-done | bytes 2097168 | tf_op jit(solution)/shard_map/all_gather | solution.py:112
  150.6 1.6 copy-done.1
  152.2 27.5 %backward_product.1 = bf16[64,256,128]{2,1,0:T(8,128)(2,1)} custom-call(s32[384]{0:T(512)S(1)} %broadcast_select_fusion.cols_ref, bf16[32,12,128,128]{3,2,1,0:T(8,128)(2,1)} %bitcast.17, bf16[32,128,256]{2,1,0:T(8,128)(2,1)S(1)} %bitcast.15), custom_call_target="tpu_custom_call" | custom-call | tf_op jit(solution)/shard_map/backward_product/pallas_call | solution.py:73
  179.7 0.0 all-reduce.2.cloned.1.call-start
  179.8 0.9 copy-done.2
  180.7 1.0 fusion
  181.7 66.2 %psum.15 = f32[256]{0:T(256)} all-reduce(f32[256]{0:T(256)S(1)} %get-tuple-element.4), channel_id=1, replica_groups=mesh['row'=16,'col'=8] {'row','col'}, use_global_device_ids=true, to_apply=%region_4.5 | all-reduce | flops 256 | bytes 2048 | tf_op jit(solution)/shard_map/psum | solution.py:111
  247.9 8.2 %reduce-scatter.5.cloned.1.call-done = bf16[4,256,128]{2,1,0:T(8,128)(2,1)} async-done(((bf16[64,256,128]{2,1,0:T(8,128)(2,1)}), bf16[4,256,128]{2,1,0:T(8,128)(2,1)}) %reduce-scatter.5.cloned.1.call-update) | async-done | bytes 262160 | tf_op jit(solution)/shard_map/reduce_scatter | solution.py:114
  256.0 1.8 copy.12
  257.8 146.6 %all-reduce.2.cloned.1.call-done = f32[256,256]{1,0:T(8,128)} async-done(((f32[256,256]{1,0:T(8,128)}), f32[256,256]{1,0:T(8,128)}) %all-reduce.2.cloned.1.call-update) | async-done | bytes 262160 | tf_op jit(solution)/shard_map/psum | solution.py:111
  404.4 1.7 copy.14
  (14 shorter events, 0.1 us)
Async XLA Ops:
  7.2 112.8 %copy-start = (bf16[256,256]{1,0:T(8,128)(2,1)S(1)}, bf16[256,256]{1,0:T(8,128)(2,1)}, u32[]{:S(2)}) copy-start(bf16[256,256]{1,0:T(8,128)(2,1)} %param.11) | copy-start | bytes 393220
  7.2 57.9 %all-gather.3.cloned.1.call-start = ((), (), s32[]{:S(2)}) async-start(), calls=%async_computation.2 | async-start | bytes 4456448 | tf_op jit(solution)/shard_map/all_gather | solution.py:98
  7.9 112.1 %reduce-scatter.3.cloned.1.call-start = ((), (), s32[]{:S(2)}) async-start(), calls=%async_computation.3 | async-start | bytes 2359296 | tf_op jit(solution)/shard_map/reduce_scatter | solution.py:100
  65.1 54.9 %copy-start.3 = (bf16[512,256]{1,0:T(8,128)(2,1)S(1)}, bf16[512,256]{1,0:T(8,128)(2,1)}, u32[]{:S(2)}) copy-start(bf16[512,256]{1,0:T(8,128)(2,1)} %param.13) | copy-start | bytes 786436
  65.1 54.9 %copy-start.4 = (f32[256]{0:T(256)S(1)}, f32[256]{0:T(256)}, u32[]{:S(2)}) copy-start(f32[256]{0:T(256)} %param.12) | copy-start | bytes 3076
  89.6 61.0 %all-gather.5.cloned.1.call-start = ((), (), s32[]{:S(2)}) async-start(), calls=%async_computation.4 | async-start | bytes 2359296 | tf_op jit(solution)/shard_map/all_gather | solution.py:112
  123.0 133.0 %reduce-scatter.5.cloned.1.call-start = ((), (), s32[]{:S(2)}) async-start(), calls=%async_computation.5 | async-start | bytes 4456448 | tf_op jit(solution)/shard_map/reduce_scatter | solution.py:114
  150.6 1.6 copy-start.1
  179.7 0.9 copy-start.2
  179.7 224.7 %all-reduce.2.cloned.1.call-start = ((), (), s32[]{:S(2)}) async-start(), calls=%async_computation.6 | async-start | bytes 524288 | tf_op jit(solution)/shard_map/psum | solution.py:111
Sparse Core Ops, SparseCore 0:
  10.2 54.8 all-gather.2
  89.7 30.2 reduce-scatter.2
  123.2 27.3 all-gather.4
  179.9 76.1 reduce-scatter.4
  261.9 142.4 all-reduce.1

commit v2 on v1

v2 whole, which is shorter than its diff:
```python
import functools

import jax
import jax.numpy as jnp
from jax import lax
from jax.experimental import pallas as pl
from jax.experimental.pallas import tpu as pltpu
from jax.sharding import PartitionSpec as P

MESH = pl.DeviceIdType.MESH
BF16, F32 = jnp.bfloat16, jnp.float32
RING = 4


def dot(a, b, dims=((1,), (0,))):
    return lax.dot_general(a, b, (dims, ((), ())), preferred_element_type=F32)


class Place:
    def __init__(self):
        row, col = lax.axis_index("row"), lax.axis_index("col")
        self.row, self.col = row, col
        self.z, self.x = row // RING, row % RING
        self.y, self.core = col // 2, col % 2

    def rows(self, dz, dx):
        return ((self.z + dz) % RING) * RING + (self.x + dx) % RING

    def cols(self, dy, other=0):
        core = 1 - self.core if other else self.core
        return ((self.y + dy) % RING) * 2 + core

    def plane(self, dz, dx):
        return (self.rows(dz, dx), self.col)

    def line(self, dy, other=0):
        return (self.row, self.cols(dy, other))


class Mail:
    def __init__(self, here, sent, came):
        self.here, self.sent, self.came, self.out = here, sent, came, []

    def make(self, number, src, dst, to):
        return pltpu.make_async_remote_copy(
            src_ref=src, dst_ref=dst, send_sem=self.sent.at[number], recv_sem=self.came.at[number],
            device_id=to, device_id_type=MESH,
        )

    def post(self, number, src, dst, to):
        copy = self.make(number, src, dst, to)
        copy.start()
        self.out.append(copy)

    def take(self, number, dst):
        self.make(number, dst, dst, (self.here.row, self.here.col)).wait_recv()

    def drain(self):
        for copy in self.out:
            copy.wait_send()


def meet(peers):
    barrier = pltpu.get_barrier_semaphore()
    for peer in peers:
        pl.semaphore_signal(barrier, inc=1, device_id=peer, device_id_type=MESH)
    pl.semaphore_wait(barrier, len(peers))


OFFSETS = (0, -1, 1, 2)


def flavour(f, dp, dq):
    return (dq, dp) if f == 0 else (dp, dq)


def gather_rows(mail, base, here, panel):
    def index(f, dp, dq):
        return here.rows(*flavour(f, dp, dq)) * 4 + 2 * f

    def number(f, slot, kind):
        return base + f * 20 + slot * 4 + kind

    def to(f, slot, d):
        return here.plane(*(flavour(f, d, 0) if slot == 0 else flavour(f, 0, d)))

    def pair(f, slot, dp):
        blocks = panel.at[pl.ds(index(f, dp, 0), 2)]
        mail.post(number(f, slot, 0), blocks, blocks, to(f, slot, 1))
        mail.post(number(f, slot, 1), blocks, blocks, to(f, slot, -1))

    def where(f, slot, d):
        return index(f, d, 0) if slot == 0 else index(f, OFFSETS[slot - 1], d)

    def onward(f, slot):
        at = where(f, slot, -1)
        mail.take(number(f, slot, 0), panel.at[pl.ds(at, 2)])
        block = panel.at[pl.ds(at, 1)]
        mail.post(number(f, slot, 2), block, block, to(f, slot, 1))
        at = where(f, slot, 1)
        mail.take(number(f, slot, 1), panel.at[pl.ds(at, 2)])
        block = panel.at[pl.ds(at + 1, 1)]
        mail.post(number(f, slot, 3), block, block, to(f, slot, -1))

    def last(f, slot):
        at = where(f, slot, 2)
        mail.take(number(f, slot, 2), panel.at[pl.ds(at, 1)])
        mail.take(number(f, slot, 3), panel.at[pl.ds(at + 1, 1)])

    both = (0, 1)
    for f in both:
        pair(f, 0, 0)
    for f in both:
        pair(f, 1, 0)
    for f in both:
        onward(f, 0)
        pair(f, 2, -1)
        pair(f, 3, 1)
    for f in both:
        onward(f, 1)
    for f in both:
        last(f, 0)
        pair(f, 4, 2)
    for slot in (2, 3, 4):
        for f in both:
            onward(f, slot)
    for slot in (1, 2, 3, 4):
        for f in both:
            last(f, slot)


GATHER_MAIL = 40
FORWARD_MAIL = GATHER_MAIL + 4 + 6 + 6 + 4


def forward_body(
    cols_ref, live_ref, features_ref, adj_hbm, weight_ref, bias_ref, upstream_ref,
    act_ref, grad_hbm, wpart_ref, bpart_ref,
    panel, adj, cross_out, cross_in, own, line_out, line_in, grads,
    sent, came, adj_sem, out_sem,
):
    here = Place()
    mail = Mail(here, sent, came)
    rows, slots, size, _ = adj.shape
    width = features_ref.shape[1]
    blocks = panel.shape[0] - 1
    piece = features_ref.shape[0]
    half = piece // 2
    per = piece // size
    parts = adj_sem.shape[0]
    step = rows // parts
    fetch = [
        pltpu.make_async_copy(adj_hbm.at[pl.ds(n * step, step)], adj.at[pl.ds(n * step, step)], adj_sem.at[n])
        for n in range(parts)
    ]
    meet([here.plane(0, 1), here.plane(0, -1), here.plane(1, 0), here.plane(-1, 0),
          here.line(1), here.line(-1), here.line(0, 1)])
    for b in range(per):
        panel[here.row * per + b] = features_ref[pl.ds(b * size, size), :]
    panel[blocks] = jnp.zeros_like(panel[blocks])
    for copy in fetch:
        copy.start()
    gather_rows(mail, 0, here, panel)
    for copy in fetch:
        copy.wait()

    def row_product(i):
        total = None
        for k in range(0, slots, 2):
            left = jnp.concatenate([adj[i, k], adj[i, k + 1]], axis=1)
            right = jnp.concatenate(
                [panel[jnp.where(s < live_ref[0, i], cols_ref[s, i], blocks)] for s in (k, k + 1)], axis=0
            )
            part = dot(left, right)
            total = part if total is None else total + part
        return total

    def piece_product(dest, store):
        @pl.loop(0, per)
        def _(n):
            store(pl.ds(pl.multiple_of(n * size, size), size), row_product(dest * per + n))

    order = (2, 1, -1, 0)
    number = GATHER_MAIL
    for n, dy in enumerate(order):
        def store(at, value, n=n):
            cross_out[n, at, :] = value.astype(BF16)

        piece_product(here.cols(dy, 1), store)
        mail.post(number + n, cross_out.at[n], cross_in.at[n], here.line(0, 1))
    for n, dy in enumerate(order):
        def store(at, value, n=n):
            own[n, at, :] = value

        piece_product(here.cols(dy), store)
    low, high = pl.ds(0, half), pl.ds(half, half)

    def chip(n, part):
        return own[n, part, :] + cross_in[n, part, :].astype(F32)

    line = number + 4
    up, down = here.line(1), here.line(-1)
    mail.take(number, cross_in.at[0])
    line_out[0] = chip(0, pl.ds(0, piece)).astype(BF16)
    mail.post(line, line_out.at[0, low], line_in.at[0], up)
    mail.post(line + 1, line_out.at[0, high], line_in.at[1], down)
    mail.take(number + 1, cross_in.at[1])
    line_out[1, high, :] = chip(1, high).astype(BF16)
    mail.post(line + 2, line_out.at[1, high], line_in.at[2], up)
    mail.take(number + 2, cross_in.at[2])
    line_out[2, low, :] = chip(2, low).astype(BF16)
    mail.post(line + 3, line_out.at[2, low], line_in.at[3], down)
    mail.take(line, line_in.at[0])
    line_out[1, low, :] = (chip(1, low) + line_in[0].astype(F32)).astype(BF16)
    mail.post(line + 4, line_out.at[1, low], line_in.at[4], up)
    mail.take(line + 1, line_in.at[1])
    line_out[2, high, :] = (chip(2, high) + line_in[1].astype(F32)).astype(BF16)
    mail.post(line + 5, line_out.at[2, high], line_in.at[5], down)
    mail.take(number + 3, cross_in.at[3])

    ring = line + 6
    across = ring + 6
    mine = here.cols(0)
    wpart = None
    bpart = None
    for part, (a, b) in enumerate(((4, 3), (2, 5))):
        at = low if part == 0 else high
        mail.take(line + a, line_in.at[a])
        mail.take(line + b, line_in.at[b])
        aggregated = (chip(3, at) + line_in[a].astype(F32) + line_in[b].astype(F32)).astype(BF16)
        preact = dot(aggregated, weight_ref[...]) + bias_ref[...]
        s = jax.nn.sigmoid(preact)
        act_ref[at, :] = (preact * s).astype(BF16)
        derivative = s * (1.0 + preact * (1.0 - s))
        grad_pre = (upstream_ref[at, :].astype(F32) * derivative).astype(BF16)
        grads[mine, at, :] = dot(grad_pre, weight_ref[...], ((1,), (1,))).astype(BF16)
        block = grads.at[mine, at]
        mail.post(ring + 2 * part, block, block, up)
        mail.post(ring + 2 * part + 1, block, block, down)
        w = dot(aggregated, grad_pre, ((0,), (0,)))
        b8 = jnp.sum(grad_pre.astype(F32).reshape(half // 8, 8, width), axis=0)
        wpart = w if wpart is None else wpart + w
        bpart = b8 if bpart is None else bpart + b8
    mail.post(across, grads.at[mine], grads.at[mine], here.line(0, 1))
    wpart_ref[...] = wpart
    bpart_ref[...] = bpart

    def out(c, n):
        copy = pltpu.make_async_copy(grads.at[c], grad_hbm.at[c], out_sem.at[n])
        copy.start()
        return copy

    copies = [out(mine, 0)]
    before, after, far = here.cols(-1), here.cols(1), here.cols(2)
    mail.take(ring, grads.at[before, low])
    block = grads.at[before, low]
    mail.post(ring + 4, block, block, up)
    mail.take(ring + 1, grads.at[after, low])
    mail.take(ring + 3, grads.at[after, high])
    block = grads.at[after, high]
    mail.post(ring + 5, block, block, down)
    mail.post(across + 1, grads.at[after], grads.at[after], here.line(0, 1))
    copies.append(out(after, 1))
    mail.take(ring + 2, grads.at[before, high])
    mail.post(across + 2, grads.at[before], grads.at[before], here.line(0, 1))
    copies.append(out(before, 2))
    mail.take(ring + 4, grads.at[far, low])
    mail.take(ring + 5, grads.at[far, high])
    mail.post(across + 3, grads.at[far], grads.at[far], here.line(0, 1))
    copies.append(out(far, 3))
    for n, dy in enumerate((0, 1, -1, 2)):
        c = here.cols(dy, 1)
        mail.take(across + n, grads.at[c])
        copies.append(out(c, 4 + n))
    for copy in copies:
        copy.wait()
    mail.drain()


def forward_layer(cols, live, features, adj, weight, bias, upstream):
    rows, slots, size, _ = adj.shape
    piece, width = features.shape
    blocks = lax.axis_size("row") * piece // size
    pieces = lax.axis_size("col")
    vmem, anywhere = pl.BlockSpec(memory_space=pltpu.VMEM), pl.BlockSpec(memory_space=pl.ANY)
    smem = pl.BlockSpec(memory_space=pltpu.SMEM)
    return pl.pallas_call(
        forward_body,
        out_shape=(
            jax.ShapeDtypeStruct((piece, width), BF16),
            jax.ShapeDtypeStruct((pieces, piece, width), BF16),
            jax.ShapeDtypeStruct((width, width), F32),
            jax.ShapeDtypeStruct((8, width), F32),
        ),
        in_specs=[smem, smem, vmem, anywhere, vmem, vmem, vmem],
        out_specs=(vmem, anywhere, vmem, vmem),
        scratch_shapes=[
            pltpu.VMEM((blocks + 1, size, width), BF16),
            pltpu.VMEM(adj.shape, BF16),
            pltpu.VMEM((4, piece, width), BF16),
            pltpu.VMEM((4, piece, width), BF16),
            pltpu.VMEM((4, piece, width), F32),
            pltpu.VMEM((3, piece, width), BF16),
            pltpu.VMEM((6, piece // 2, width), BF16),
            pltpu.VMEM((pieces, piece, width), BF16),
            pltpu.SemaphoreType.DMA((FORWARD_MAIL,)),
            pltpu.SemaphoreType.DMA((FORWARD_MAIL,)),
            pltpu.SemaphoreType.DMA((4,)),
            pltpu.SemaphoreType.DMA((8,)),
        ],
        compiler_params=pltpu.CompilerParams(
            collective_id=0, has_side_effects=True, vmem_limit_bytes=56 << 20
        ),
        name="forward_layer",
    )(cols, live, features, adj, weight, bias, upstream)


def backward_body(cols_ref, live_ref, adj_ref, grad_ref, out_ref, acc_ref):
    i = pl.program_id(0)
    slots, size = adj_ref.shape[1], adj_ref.shape[3]
    blocks = out_ref.shape[0]

    @pl.when(i == 0)
    def _():
        acc_ref[...] = jnp.zeros_like(acc_ref)

    turned = grad_ref[0].T
    for k in range(0, slots, 2):
        right = jnp.concatenate([adj_ref[0, k], adj_ref[0, k + 1]], axis=1)
        part = dot(turned, right)
        for s in (0, 1):
            j = jnp.where(k + s < live_ref[0, i], cols_ref[k + s, i], blocks)
            acc_ref[j] += part[:, s * size : (s + 1) * size]

    @pl.when(i == pl.num_programs(0) - 1)
    def _():
        @pl.loop(0, out_ref.shape[0])
        def _(j):
            out_ref[j] = acc_ref[j].astype(out_ref.dtype)


def backward_product(cols, live, adj, grad, blocks):
    rows, slots, size, _ = adj.shape
    width = grad.shape[2]
    return pl.pallas_call(
        backward_body,
        out_shape=jax.ShapeDtypeStruct((blocks, width, size), BF16),
        grid_spec=pltpu.PrefetchScalarGridSpec(
            num_scalar_prefetch=2,
            grid=(rows,),
            in_specs=[
                pl.BlockSpec((1, slots, size, size), lambda i, c, l: (i, 0, 0, 0)),
                pl.BlockSpec((1, size, width), lambda i, c, l: (i, 0, 0)),
            ],
            out_specs=pl.BlockSpec((blocks, width, size), lambda i, c, l: (0, 0, 0)),
            scratch_shapes=[pltpu.VMEM((blocks + 1, width, size), F32)],
        ),
        compiler_params=pltpu.CompilerParams(vmem_limit_bytes=48 << 20),
        name="backward_product",
    )(cols, live, adj, grad)


SCATTER_MAIL = 60
LINE_MAIL, SLICE_MAIL = 7, 3
BACK_MAIL = SCATTER_MAIL + 2 * LINE_MAIL + 3 * SLICE_MAIL


def back_body(
    turned_ref, wpart_ref, bpart_ref, feature_grad_ref, wgrad_ref, bgrad_ref,
    rx, tx, stage, w_out, w_in, x_out, x_in, z_in, slab, sent, came,
):
    here = Place()
    mail = Mail(here, sent, came)
    size = turned_ref.shape[2]
    nx = w_out.shape[0]
    slice_rows = wpart_ref.shape[0] // nx
    thin = slice_rows // RING
    peers = [here.plane(0, 1), here.plane(0, -1), here.plane(0, 2), here.plane(1, 0), here.plane(-1, 0), here.plane(2, 0)]
    peers += [(here.row, (here.col + d) % nx) for d in range(1, nx)]
    meet(peers)

    for d in range(1, nx):
        c = (here.col + d) % nx
        w_out[c, :slice_rows] = wpart_ref[pl.ds(c * slice_rows, slice_rows), :]
        w_out[c, slice_rows:] = bpart_ref[...]
    w_in[here.col, :slice_rows] = wpart_ref[pl.ds(here.col * slice_rows, slice_rows), :]
    w_in[here.col, slice_rows:] = bpart_ref[...]
    base = SCATTER_MAIL
    for d in range(1, nx):
        c = (here.col + d) % nx
        mail.post(base + d - 1, w_out.at[c], w_in.at[here.col], (here.row, c))

    def number(f, slot, kind):
        return f * 30 + slot * 6 + kind

    def to(f, slot, d):
        return here.plane(*(flavour(f, d, 0) if slot < 4 else flavour(f, 0, d)))

    def source(f, slot, d, b):
        if slot < 4:
            return turned_ref.at[here.rows(*flavour(f, d, OFFSETS[slot])) * 4 + 2 * f + b]
        return stage.at[f, OFFSETS.index(d), b]

    def send(f, slot, kind, d, b):
        n = number(f, slot, kind)
        if slot < 4:
            src = source(f, slot, 2 if kind < 2 else d, b)
        else:
            src = tx.at[n]
            tx[n] = source(f, slot, 2 if kind < 2 else d, b)[...].astype(BF16)
        mail.post(n, src, rx.at[n], to(f, slot, d))

    def first(f, slot):
        send(f, slot, 0, 1, 0)
        send(f, slot, 1, -1, 1)

    def direct(f, slot):
        send(f, slot, 2, 1, 1)
        send(f, slot, 3, -1, 0)

    def onward(f, slot):
        for kind, d, b in ((0, 1, 0), (1, -1, 1)):
            mail.take(number(f, slot, kind), rx.at[number(f, slot, kind)])
            n = number(f, slot, 4 + kind)
            tx[n] = (source(f, slot, d, b)[...].astype(F32) + rx[number(f, slot, kind)].astype(F32)).astype(BF16)
            mail.post(n, tx.at[n], rx.at[n], to(f, slot, d))

    def total(f, slot, b):
        result = source(f, slot, 0, b)[...].astype(F32)
        for kind in ((4, 3) if b == 0 else (2, 5)):
            n = number(f, slot, kind)
            mail.take(n, rx.at[n])
            result = result + rx[n].astype(F32)
        return result

    both = (0, 1)
    order = (3, 1, 2, 0)
    for slot in order:
        for f in both:
            first(f, slot)
    for slot in order:
        for f in both:
            direct(f, slot)

    def finish(slot):
        for f in both:
            for b in (0, 1):
                stage[f, slot, b] = total(f, slot, b)

    for f in both:
        onward(f, 3)
    for d in range(1, nx):
        mail.take(base + d - 1, w_in.at[(here.col + nx - d) % nx])
    got = w_in[0]
    for c in range(1, nx):
        got = got + w_in[c]
    second = base + nx - 1
    for n in range(RING):
        x_out[n, :thin] = got[n * thin : (n + 1) * thin]
        x_out[n, thin:] = got[slice_rows:]
    x_in[here.x] = x_out[here.x]
    for d in range(1, RING):
        x = (here.x + d) % RING
        mail.post(second + d - 1, x_out.at[x], x_in.at[here.x], here.plane(0, d))
    for f in both:
        onward(f, 1)
        onward(f, 2)
    finish(3)
    for f in both:
        first(f, 4)
    for f in both:
        onward(f, 0)
    for d in range(1, RING):
        mail.take(second + d - 1, x_in.at[(here.x + RING - d) % RING])
    got = x_in[0]
    for n in range(1, RING):
        got = got + x_in[n]
    z_in[here.z] = got
    third = second + SLICE_MAIL
    for d in range(1, RING):
        mail.post(third + d - 1, z_in.at[here.z], z_in.at[here.z], here.plane(d, 0))
    finish(1)
    finish(2)
    for f in both:
        direct(f, 4)
    for f in both:
        onward(f, 4)
    for d in range(1, RING):
        mail.take(third + d - 1, z_in.at[(here.z + RING - d) % RING])
    got = z_in[0]
    for n in range(1, RING):
        got = got + z_in[n]
    bgrad_ref[...] = jnp.sum(got[thin:], axis=0, keepdims=True)
    slab[here.x] = got[:thin]
    fourth = third + SLICE_MAIL
    for d in range(1, RING):
        mail.post(fourth + d - 1, slab.at[here.x], slab.at[here.x], here.plane(0, d))
    finish(0)
    for d in range(1, RING):
        mail.take(fourth + d - 1, slab.at[(here.x + RING - d) % RING])
    fifth = fourth + SLICE_MAIL
    w_out[here.col, :slice_rows] = slab[...].reshape(slice_rows, slab.shape[2])
    wgrad_ref[pl.ds(here.col * slice_rows, slice_rows), :] = w_out[here.col, :slice_rows]
    for d in range(1, nx):
        part = wgrad_ref.at[pl.ds(here.col * slice_rows, slice_rows)]
        mail.post(fifth + d - 1, part, part, (here.row, (here.col + d) % nx))
    for f in both:
        for b in (0, 1):
            feature_grad_ref[pl.ds((2 * f + b) * size, size), :] = total(f, 4, b).T.astype(BF16)
    for d in range(1, nx):
        c = (here.col + nx - d) % nx
        mail.take(fifth + d - 1, wgrad_ref.at[pl.ds(c * slice_rows, slice_rows)])
    mail.drain()


def back_sums(turned, wpart, bpart, piece):
    _, width, size = turned.shape
    nx = lax.axis_size("col")
    slice_rows = width // nx
    vmem = pl.BlockSpec(memory_space=pltpu.VMEM)
    return pl.pallas_call(
        back_body,
        out_shape=(
            jax.ShapeDtypeStruct((piece, width), BF16),
            jax.ShapeDtypeStruct((width, width), F32),
            jax.ShapeDtypeStruct((1, width), F32),
        ),
        in_specs=[vmem, vmem, vmem],
        out_specs=(vmem, vmem, vmem),
        scratch_shapes=[
            pltpu.VMEM((60, width, size), BF16),
            pltpu.VMEM((60, width, size), BF16),
            pltpu.VMEM((2, 4, 2, width, size), F32),
            pltpu.VMEM((nx, slice_rows + 8, width), F32),
            pltpu.VMEM((nx, slice_rows + 8, width), F32),
            pltpu.VMEM((RING, slice_rows // RING + 8, width), F32),
            pltpu.VMEM((RING, slice_rows // RING + 8, width), F32),
            pltpu.VMEM((RING, slice_rows // RING + 8, width), F32),
            pltpu.VMEM((RING, slice_rows // RING, width), F32),
            pltpu.SemaphoreType.DMA((BACK_MAIL,)),
            pltpu.SemaphoreType.DMA((BACK_MAIL,)),
        ],
        compiler_params=pltpu.CompilerParams(
            collective_id=1, has_side_effects=True, vmem_limit_bytes=48 << 20
        ),
        name="back_sums",
    )(turned, wpart, bpart)


def local(features, adjacency, block_cols, block_live, weight, bias, upstream):
    rows, _, slots, size, _ = adjacency.shape
    piece, width = features.shape
    adj = adjacency.reshape(rows, slots, size, size)
    blocks = piece * lax.axis_size("row") // size
    cols = block_cols.reshape(rows, slots).T
    live = block_live.reshape(1, rows)
    act, grads, wpart, bpart = forward_layer(
        cols, live, features, adj, weight, bias.reshape(1, width), upstream
    )
    turned = backward_product(cols, live, adj, grads.reshape(rows, size, width), blocks)
    feature_grad, wgrad, bgrad = back_sums(turned, wpart, bpart, piece)
    return act, feature_grad, wgrad, bgrad.reshape(width)


def solution(mesh):
    placed = (
        P(("col", "row"), None),
        P("row", "col", None, None, None),
        P("row", "col", None),
        P("row", "col"),
        P(),
        P(),
        P(("row", "col"), None),
    )
    return jax.shard_map(
        local,
        mesh=mesh,
        in_specs=placed,
        out_specs=(P(("row", "col"), None), P(("col", "row"), None), P(), P()),
        check_vma=False,
    )
```

time: 414 us -> 139 us (0.34)
  waiting for transfers between devices: 269 us -> 0 us
  Pallas kernels: 52 us -> 130 us
  blocking collectives: 66.2 us -> 0 us
  between operations: 13.8 us -> 0.69 us
    psum x1 -> x0, waiting for transfers between devices: 147 us -> none  [local(): weight_grad, bias_grad = lax.psum((weight_part, bias_part), ('row', 'col'))]
    all_gather x2 -> x0, waiting for transfers between devices: 82.8 us -> none  [the longest x1 55.4 us: local(): lax.all_gather(features, 'row', axis=0, tiled=True)]
    pallas_call x1 -> x2, Pallas kernels: 24.5 us -> 102 us  [the longest x1 66 us: forward_layer(): pl.pallas_call(forward_body, out_shape=(jax.ShapeDtypeStruct((piece, widt...]
    psum x1 -> x0, blocking collectives: 66.2 us -> none  [local(): weight_grad, bias_grad = lax.psum((weight_part, bias_part), ('row', 'col'))]
    reduce_scatter x2 -> x0, waiting for transfers between devices: 38.5 us -> none  [the longest x1 30.4 us: local(): lax.psum_scatter(partial, 'col', scatter_dimension=0, tiled=True)]
  transfers between devices with their start and end apart: 5 -> 0, of which waited for: 5 -> 0; matrix products, arithmetic and copies ran while one was open for 1% -> 0% of each run, Pallas kernels for 0% -> 0%
where the time goes in v2:
time: 139 us; the launch traced here: 138 us
  Pallas kernels  130 us (94%)
  local copies, waits for them, and re-layouts  7.75 us (6%)
    pallas_call x1, Pallas kernels, forward_layer(): pl.pallas_call(forward_body, out_shape=(jax.ShapeDtypeStruct((piece, widt...  66 us
    pallas_call x1, Pallas kernels, back_sums(): pl.pallas_call(back_body, out_shape=(jax.ShapeDtypeStruct((piece, width),...  36 us
    pallas_call x1, Pallas kernels, backward_product(): pl.pallas_call(backward_body, out_shape=jax.ShapeDtypeStruct((blocks, wid...  27.7 us
    unnamed x19, local copies, waits for them, and re-layouts  7.75 us

profile of v2, /device:TPU:1, one launch (start us, length us, event | category | flops | bytes accessed | tf_op | source)
XLA Modules:
  0.0 138.1 jit_solution(11664435617283524664)
XLA Ops:
  0.6 1.3 copy.13
  1.9 0.0 copy-start.3
  1.9 0.0 copy-start.5
  1.9 66.0 %forward_layer.1 = (bf16[512,256]{1,0:T(8,128)(2,1)}, bf16[8,512,256]{2,1,0:T(8,128)(2,1)}, f32[256,256]{1,0:T(8,128)}, f32[8,256]{1,0:T(8,128)}) custom-call(s32[12,32]{1,0:T(8,128)} %bitcast.11, s32[1,32]{1,0:T(1,128)} %bitcast.13, bf16[512,256]{1,0:T(8,128)(2,1)} %features_ref.1, bf16[32,12,128,128]{3,2,1,0:T(8,128)(2,1)} %bitcast.16, ...), custom_call_target="tpu_custom_call" | custom-call | tf_op jit(solution)/shard_map/forward_layer/pallas_call | solution.py:287
  68.0 0.0 copy-done.3
  68.0 0.0 copy-done.5
  68.0 0.0 copy-start.1
  68.0 1.6 %copy-done.1 = bf16[8,512,256]{2,1,0:T(8,128)(2,1)S(1)} copy-done((bf16[8,512,256]{2,1,0:T(8,128)(2,1)S(1)}, bf16[8,512,256]{2,1,0:T(8,128)(2,1)}, u32[]{:S(2)}) %copy-start.1) | copy-done | bytes 2097176
  69.6 0.0 copy-start.2
  69.6 0.0 copy-start.4
  69.6 27.7 %backward_product.1.turned_ref = bf16[64,256,128]{2,1,0:T(8,128)(2,1)} custom-call(s32[12,32]{1,0:T(8,128)S(1)} %bitcast.12, s32[1,32]{1,0:T(1,128)S(1)} %bitcast.14, bf16[32,12,128,128]{3,2,1,0:T(8,128)(2,1)} %bitcast.17, bf16[32,128,256]{2,1,0:T(8,128)(2,1)S(1)} %bitcast.10), custom_call_target="tpu_custom_call" | custom-call | tf_op jit(solution)/shard_map/backward_product/pallas_call | solution.py:345
  97.3 0.0 copy-done.2
  97.3 0.0 copy-done.4
  97.3 0.0 copy-start
  97.3 2.2 %copy-done = bf16[64,256,128]{2,1,0:T(8,128)(2,1)S(1)} copy-done((bf16[64,256,128]{2,1,0:T(8,128)(2,1)S(1)}, bf16[64,256,128]{2,1,0:T(8,128)(2,1)}, u32[]{:S(2)}) %copy-start) | copy-done | bytes 4194328
  99.4 0.0 copy-start.6
  99.4 36.0 %back_sums.1 = (bf16[512,256]{1,0:T(8,128)(2,1)S(1)}, f32[256,256]{1,0:T(8,128)S(1)}, f32[1,256]{1,0:T(1,128)S(1)}) custom-call(bf16[64,256,128]{2,1,0:T(8,128)(2,1)S(1)} %copy-done, f32[256,256]{1,0:T(8,128)S(1)} %copy-done.2, f32[8,256]{1,0:T(8,128)S(1)} %copy-done.4), custom_call_target="tpu_custom_call" | custom-call | tf_op jit(solution)/shard_map/back_sums/pallas_call | solution.py:521
  135.4 0.0 copy-done.6
  135.4 0.7 copy.18
  136.2 0.7 copy.19
  136.9 0.7 copy.20
  137.6 0.6 copy.21
Async XLA Ops:
  1.9 66.1 %copy-start.3 = (s32[32,1,12]{0,2,1:T(8,128)S(1)}, s32[32,1,12]{0,2,1:T(8,128)}, u32[]{:S(2)}) copy-start(s32[32,1,12]{0,2,1:T(8,128)} %copy.13) | copy-start | bytes 4612
  1.9 66.1 %copy-start.5 = (s32[32,1]{0,1:T(1,128)S(1)}, s32[32,1]{0,1:T(1,128)}, u32[]{:S(2)}) copy-start(s32[32,1]{0,1:T(1,128)} %param.10) | copy-start | bytes 388
  68.0 1.6 %copy-start.1 = (bf16[8,512,256]{2,1,0:T(8,128)(2,1)S(1)}, bf16[8,512,256]{2,1,0:T(8,128)(2,1)}, u32[]{:S(2)}) copy-start(bf16[8,512,256]{2,1,0:T(8,128)(2,1)} %get-tuple-element.12) | copy-start | bytes 6291460
  69.6 27.7 %copy-start.2 = (f32[256,256]{1,0:T(8,128)S(1)}, f32[256,256]{1,0:T(8,128)}, u32[]{:S(2)}) copy-start(f32[256,256]{1,0:T(8,128)} %get-tuple-element.13.wpart_ref) | copy-start | bytes 786436
  69.6 27.7 %copy-start.4 = (f32[8,256]{1,0:T(8,128)S(1)}, f32[8,256]{1,0:T(8,128)}, u32[]{:S(2)}) copy-start(f32[8,256]{1,0:T(8,128)} %get-tuple-element.14.bpart_ref) | copy-start | bytes 24580
  97.3 2.2 %copy-start = (bf16[64,256,128]{2,1,0:T(8,128)(2,1)S(1)}, bf16[64,256,128]{2,1,0:T(8,128)(2,1)}, u32[]{:S(2)}) copy-start(bf16[64,256,128]{2,1,0:T(8,128)(2,1)} %backward_product.1.turned_ref) | copy-start | bytes 12582916
  99.4 36.0 %copy-start.6 = (bf16[512,256]{1,0:T(8,128)(2,1)S(1)}, bf16[512,256]{1,0:T(8,128)(2,1)}, u32[]{:S(2)}) copy-start(bf16[512,256]{1,0:T(8,128)(2,1)} %get-tuple-element.22) | copy-start | bytes 786436

commit v3 on v2

--- a/solution.py
+++ b/solution.py
@@ -130,7 +130,8 @@
 
 
 GATHER_MAIL = 40
-FORWARD_MAIL = GATHER_MAIL + 4 + 6 + 6 + 4
+FORWARD_MAIL = GATHER_MAIL + 4 + 6 + 6 + 5
+EXTRA = 8
 
 
 def forward_body(
@@ -169,30 +170,27 @@
         for k in range(0, slots, 2):
             left = jnp.concatenate([adj[i, k], adj[i, k + 1]], axis=1)
             right = jnp.concatenate(
-                [panel[jnp.where(s < live_ref[0, i], cols_ref[s, i], blocks)] for s in (k, k + 1)], axis=0
+                [panel[jnp.where(s < live_ref[0, i], cols_ref[s, 0, i], blocks)] for s in (k, k + 1)], axis=0
             )
             part = dot(left, right)
             total = part if total is None else total + part
         return total
 
-    def piece_product(dest, store):
-        @pl.loop(0, per)
-        def _(n):
-            store(pl.ds(pl.multiple_of(n * size, size), size), row_product(dest * per + n))
-
-    order = (2, 1, -1, 0)
+    def piece_product(dest, out):
+        for n in range(per):
+            out[n * size : (n + 1) * size, :] = row_product(dest * per + n).astype(out.dtype)
+
     number = GATHER_MAIL
-    for n, dy in enumerate(order):
-        def store(at, value, n=n):
-            cross_out[n, at, :] = value.astype(BF16)
-
-        piece_product(here.cols(dy, 1), store)
+    offsets = (2, 1, -1, 0)
+
+    def cross(n):
+        piece_product(here.cols(offsets[n], 1), cross_out.at[n])
         mail.post(number + n, cross_out.at[n], cross_in.at[n], here.line(0, 1))
-    for n, dy in enumerate(order):
-        def store(at, value, n=n):
-            own[n, at, :] = value
-
-        piece_product(here.cols(dy), store)
+
+    def keep(n):
+        piece_product(here.cols(offsets[n]), own.at[n])
+        mail.take(number + n, cross_in.at[n])
+
     low, high = pl.ds(0, half), pl.ds(half, half)
 
     def chip(n, part):
@@ -200,14 +198,18 @@
 
     line = number + 4
     up, down = here.line(1), here.line(-1)
-    mail.take(number, cross_in.at[0])
+    cross(0)
+    cross(1)
+    keep(0)
     line_out[0] = chip(0, pl.ds(0, piece)).astype(BF16)
     mail.post(line, line_out.at[0, low], line_in.at[0], up)
     mail.post(line + 1, line_out.at[0, high], line_in.at[1], down)
-    mail.take(number + 1, cross_in.at[1])
+    cross(2)
+    keep(1)
     line_out[1, high, :] = chip(1, high).astype(BF16)
     mail.post(line + 2, line_out.at[1, high], line_in.at[2], up)
-    mail.take(number + 2, cross_in.at[2])
+    cross(3)
+    keep(2)
     line_out[2, low, :] = chip(2, low).astype(BF16)
     mail.post(line + 3, line_out.at[2, low], line_in.at[3], down)
     mail.take(line, line_in.at[0])
@@ -216,7 +218,7 @@
     mail.take(line + 1, line_in.at[1])
     line_out[2, high, :] = (chip(2, high) + line_in[1].astype(F32)).astype(BF16)
     mail.post(line + 5, line_out.at[2, high], line_in.at[5], down)
-    mail.take(number + 3, cross_in.at[3])
+    keep(3)
 
     ring = line + 6
     across = ring + 6
@@ -264,13 +266,17 @@
     mail.take(ring + 2, grads.at[before, high])
     mail.post(across + 2, grads.at[before], grads.at[before], here.line(0, 1))
     copies.append(out(before, 2))
-    mail.take(ring + 4, grads.at[far, low])
-    mail.take(ring + 5, grads.at[far, high])
-    mail.post(across + 3, grads.at[far], grads.at[far], here.line(0, 1))
+    for n, at in enumerate((low, high)):
+        mail.take(ring + 4 + n, grads.at[far, at])
+        mail.post(across + 3 + n, grads.at[far, at], grads.at[far, at], here.line(0, 1))
     copies.append(out(far, 3))
     for n, dy in enumerate((0, 1, -1, 2)):
         c = here.cols(dy, 1)
-        mail.take(across + n, grads.at[c])
+        if n < 3:
+            mail.take(across + n, grads.at[c])
+        else:
+            mail.take(across + 3, grads.at[c, low])
+            mail.take(across + 4, grads.at[c, high])
         copies.append(out(c, 4 + n))
     for copy in copies:
         copy.wait()
@@ -315,49 +321,73 @@
     )(cols, live, features, adj, weight, bias, upstream)
 
 
-def backward_body(cols_ref, live_ref, adj_ref, grad_ref, out_ref, acc_ref):
-    i = pl.program_id(0)
-    slots, size = adj_ref.shape[1], adj_ref.shape[3]
-    blocks = out_ref.shape[0]
-
-    @pl.when(i == 0)
-    def _():
-        acc_ref[...] = jnp.zeros_like(acc_ref)
-
-    turned = grad_ref[0].T
-    for k in range(0, slots, 2):
-        right = jnp.concatenate([adj_ref[0, k], adj_ref[0, k + 1]], axis=1)
-        part = dot(turned, right)
-        for s in (0, 1):
-            j = jnp.where(k + s < live_ref[0, i], cols_ref[k + s, i], blocks)
-            acc_ref[j] += part[:, s * size : (s + 1) * size]
-
-    @pl.when(i == pl.num_programs(0) - 1)
-    def _():
-        @pl.loop(0, out_ref.shape[0])
-        def _(j):
-            out_ref[j] = acc_ref[j].astype(out_ref.dtype)
-
-
-def backward_product(cols, live, adj, grad, blocks):
+PARTS = 4
+
+
+def backward_body(
+    cols_ref, live_ref, adj_hbm, grad_hbm, act_hbm, out, act_out_hbm, adj, grad, acc, in_sem, act_sem
+):
+    rows, slots, size, _ = adj.shape
+    blocks = out.shape[0]
+    step, group = rows // PARTS, blocks // PARTS
+
+    def fetch(n):
+        at = pl.ds(n * step, step)
+        return (
+            pltpu.make_async_copy(adj_hbm.at[at], adj.at[at], in_sem.at[0, n]),
+            pltpu.make_async_copy(grad_hbm.at[at], grad.at[at], in_sem.at[1, n]),
+        )
+
+    for n in range(PARTS):
+        for copy in fetch(n):
+            copy.start()
+    passing = pltpu.make_async_copy(act_hbm, act_out_hbm, act_sem)
+    passing.start()
+
+    @pl.loop(0, blocks)
+    def _(j):
+        acc[j] = jnp.zeros_like(acc[j])
+
+    @pl.loop(0, PARTS)
+    def _(n):
+        for copy in fetch(n):
+            copy.wait()
+        for u in range(step):
+            i = n * step + u
+            for k in range(slots):
+                j = jnp.where(k < live_ref[0, i], cols_ref[k, 0, i], blocks)
+                acc[j] += dot(adj[i, k], grad[i], ((0,), (0,)))
+
+    @pl.loop(0, PARTS)
+    def _(n):
+        for u in range(group):
+            out[n * group + u] = acc[n * group + u].astype(out.dtype)
+
+    passing.wait()
+
+
+def backward_product(cols, live, adj, grad, act, blocks):
     rows, slots, size, _ = adj.shape
     width = grad.shape[2]
+    vmem, smem, anywhere = pl.BlockSpec(memory_space=pltpu.VMEM), pl.BlockSpec(memory_space=pltpu.SMEM), pl.BlockSpec(memory_space=pl.ANY)
     return pl.pallas_call(
         backward_body,
-        out_shape=jax.ShapeDtypeStruct((blocks, width, size), BF16),
-        grid_spec=pltpu.PrefetchScalarGridSpec(
-            num_scalar_prefetch=2,
-            grid=(rows,),
-            in_specs=[
-                pl.BlockSpec((1, slots, size, size), lambda i, c, l: (i, 0, 0, 0)),
-                pl.BlockSpec((1, size, width), lambda i, c, l: (i, 0, 0)),
-            ],
-            out_specs=pl.BlockSpec((blocks, width, size), lambda i, c, l: (0, 0, 0)),
-            scratch_shapes=[pltpu.VMEM((blocks + 1, width, size), F32)],
+        out_shape=(
+            jax.ShapeDtypeStruct((blocks, size, width), BF16),
+            jax.ShapeDtypeStruct(act.shape, BF16),
         ),
-        compiler_params=pltpu.CompilerParams(vmem_limit_bytes=48 << 20),
+        in_specs=[smem, smem, anywhere, anywhere, anywhere],
+        out_specs=(vmem, anywhere),
+        scratch_shapes=[
+            pltpu.VMEM(adj.shape, BF16),
+            pltpu.VMEM(grad.shape, BF16),
+            pltpu.VMEM((blocks + 1, size, width), F32),
+            pltpu.SemaphoreType.DMA((2, PARTS)),
+            pltpu.SemaphoreType.DMA,
+        ],
+        compiler_params=pltpu.CompilerParams(vmem_limit_bytes=40 << 20),
         name="backward_product",
-    )(cols, live, adj, grad)
+    )(cols, live, adj, grad, act)
 
 
 SCATTER_MAIL = 60
@@ -366,25 +396,24 @@
 
 
 def back_body(
-    turned_ref, wpart_ref, bpart_ref, feature_grad_ref, wgrad_ref, bgrad_ref,
+    sums_ref, wpart_ref, bpart_ref, feature_grad_ref, wgrad_ref, bgrad_ref,
     rx, tx, stage, w_out, w_in, x_out, x_in, z_in, slab, sent, came,
 ):
     here = Place()
     mail = Mail(here, sent, came)
-    size = turned_ref.shape[2]
+    size = sums_ref.shape[1]
     nx = w_out.shape[0]
     slice_rows = wpart_ref.shape[0] // nx
     thin = slice_rows // RING
-    peers = [here.plane(0, 1), here.plane(0, -1), here.plane(0, 2), here.plane(1, 0), here.plane(-1, 0), here.plane(2, 0)]
+    peers = [here.plane(*at) for at in ((0, 1), (0, -1), (0, 2), (1, 0), (-1, 0), (2, 0))]
     peers += [(here.row, (here.col + d) % nx) for d in range(1, nx)]
-    meet(peers)
-
     for d in range(1, nx):
         c = (here.col + d) % nx
         w_out[c, :slice_rows] = wpart_ref[pl.ds(c * slice_rows, slice_rows), :]
         w_out[c, slice_rows:] = bpart_ref[...]
     w_in[here.col, :slice_rows] = wpart_ref[pl.ds(here.col * slice_rows, slice_rows), :]
     w_in[here.col, slice_rows:] = bpart_ref[...]
+    meet(peers)
     base = SCATTER_MAIL
     for d in range(1, nx):
         c = (here.col + d) % nx
@@ -398,7 +427,7 @@
 
     def source(f, slot, d, b):
         if slot < 4:
-            return turned_ref.at[here.rows(*flavour(f, d, OFFSETS[slot])) * 4 + 2 * f + b]
+            return sums_ref.at[here.rows(*flavour(f, d, OFFSETS[slot])) * 4 + 2 * f + b]
         return stage.at[f, OFFSETS.index(d), b]
 
     def send(f, slot, kind, d, b):
@@ -434,87 +463,99 @@
         return result
 
     both = (0, 1)
-    order = (3, 1, 2, 0)
-    for slot in order:
-        for f in both:
-            first(f, slot)
-    for slot in order:
-        for f in both:
-            direct(f, slot)
 
     def finish(slot):
         for f in both:
             for b in (0, 1):
                 stage[f, slot, b] = total(f, slot, b)
 
-    for f in both:
-        onward(f, 3)
-    for d in range(1, nx):
-        mail.take(base + d - 1, w_in.at[(here.col + nx - d) % nx])
-    got = w_in[0]
-    for c in range(1, nx):
-        got = got + w_in[c]
     second = base + nx - 1
-    for n in range(RING):
-        x_out[n, :thin] = got[n * thin : (n + 1) * thin]
-        x_out[n, thin:] = got[slice_rows:]
-    x_in[here.x] = x_out[here.x]
-    for d in range(1, RING):
-        x = (here.x + d) % RING
-        mail.post(second + d - 1, x_out.at[x], x_in.at[here.x], here.plane(0, d))
-    for f in both:
-        onward(f, 1)
-        onward(f, 2)
+    third = second + SLICE_MAIL
+    fourth = third + SLICE_MAIL
+    fifth = fourth + SLICE_MAIL
+
+    def added(parts, count):
+        got = parts[0]
+        for n in range(1, count):
+            got = got + parts[n]
+        return got
+
+    def column_sums():
+        for d in range(1, nx):
+            mail.take(base + d - 1, w_in.at[(here.col + nx - d) % nx])
+        got = added(w_in, nx)
+        for n in range(RING):
+            x_out[n, :thin] = got[n * thin : (n + 1) * thin]
+            x_out[n, thin:] = got[slice_rows:]
+        x_in[here.x] = x_out[here.x]
+        for d in range(1, RING):
+            mail.post(second + d - 1, x_out.at[(here.x + d) % RING], x_in.at[here.x], here.plane(0, d))
+
+    def x_sums():
+        for d in range(1, RING):
+            mail.take(second + d - 1, x_in.at[(here.x + RING - d) % RING])
+        z_in[here.z] = added(x_in, RING)
+        for d in range(1, RING):
+            mail.post(third + d - 1, z_in.at[here.z], z_in.at[here.z], here.plane(d, 0))
+
+    def z_sums():
+        for d in range(1, RING):
+            mail.take(third + d - 1, z_in.at[(here.z + RING - d) % RING])
+        got = added(z_in, RING)
+        bgrad_ref[...] = jnp.sum(got[thin:], axis=0, keepdims=True)
+        slab[here.x] = got[:thin]
+        for d in range(1, RING):
+            mail.post(fourth + d - 1, slab.at[here.x], slab.at[here.x], here.plane(0, d))
+
+    mine = pl.ds(here.col * slice_rows, slice_rows)
+
+    def spread():
+        for d in range(1, RING):
+            mail.take(fourth + d - 1, slab.at[(here.x + RING - d) % RING])
+        for n in range(RING):
+            wgrad_ref[pl.ds(here.col * slice_rows + n * thin, thin), :] = slab[n]
+        for d in range(1, nx):
+            mail.post(fifth + d - 1, wgrad_ref.at[mine], wgrad_ref.at[mine], (here.row, (here.col + d) % nx))
+
+    def each(action, *slots):
+        for slot in slots:
+            for f in both:
+                action(f, slot)
+
+    each(first, 3)
+    each(direct, 3)
+    each(first, 1)
+    each(onward, 3)
+    each(first, 2)
+    column_sums()
+    each(onward, 1)
+    each(direct, 1)
+    x_sums()
+    each(onward, 2)
+    each(direct, 2)
     finish(3)
-    for f in both:
-        first(f, 4)
-    for f in both:
-        onward(f, 0)
-    for d in range(1, RING):
-        mail.take(second + d - 1, x_in.at[(here.x + RING - d) % RING])
-    got = x_in[0]
-    for n in range(1, RING):
-        got = got + x_in[n]
-    z_in[here.z] = got
-    third = second + SLICE_MAIL
-    for d in range(1, RING):
-        mail.post(third + d - 1, z_in.at[here.z], z_in.at[here.z], here.plane(d, 0))
+    each(first, 4)
+    each(first, 0)
+    z_sums()
+    each(direct, 0)
     finish(1)
     finish(2)
-    for f in both:
-        direct(f, 4)
-    for f in both:
-        onward(f, 4)
-    for d in range(1, RING):
-        mail.take(third + d - 1, z_in.at[(here.z + RING - d) % RING])
-    got = z_in[0]
-    for n in range(1, RING):
-        got = got + z_in[n]
-    bgrad_ref[...] = jnp.sum(got[thin:], axis=0, keepdims=True)
-    slab[here.x] = got[:thin]
-    fourth = third + SLICE_MAIL
-    for d in range(1, RING):
-        mail.post(fourth + d - 1, slab.at[here.x], slab.at[here.x], here.plane(0, d))
+    each(onward, 4)
+    each(direct, 4)
+    spread()
+    each(onward, 0)
     finish(0)
-    for d in range(1, RING):
-        mail.take(fourth + d - 1, slab.at[(here.x + RING - d) % RING])
-    fifth = fourth + SLICE_MAIL
-    w_out[here.col, :slice_rows] = slab[...].reshape(slice_rows, slab.shape[2])
-    wgrad_ref[pl.ds(here.col * slice_rows, slice_rows), :] = w_out[here.col, :slice_rows]
-    for d in range(1, nx):
-        part = wgrad_ref.at[pl.ds(here.col * slice_rows, slice_rows)]
-        mail.post(fifth + d - 1, part, part, (here.row, (here.col + d) % nx))
     for f in both:
         for b in (0, 1):
-            feature_grad_ref[pl.ds((2 * f + b) * size, size), :] = total(f, 4, b).T.astype(BF16)
+            feature_grad_ref[pl.ds((2 * f + b) * size, size), :] = total(f, 4, b).astype(BF16)
     for d in range(1, nx):
         c = (here.col + nx - d) % nx
         mail.take(fifth + d - 1, wgrad_ref.at[pl.ds(c * slice_rows, slice_rows)])
     mail.drain()
 
 
-def back_sums(turned, wpart, bpart, piece):
-    _, width, size = turned.shape
+def back_sums(sums, wpart, bpart, piece):
+    _, size, width = sums.shape
     nx = lax.axis_size("col")
     slice_rows = width // nx
     vmem = pl.BlockSpec(memory_space=pltpu.VMEM)
@@ -528,23 +569,39 @@
         in_specs=[vmem, vmem, vmem],
         out_specs=(vmem, vmem, vmem),
         scratch_shapes=[
-            pltpu.VMEM((60, width, size), BF16),
-            pltpu.VMEM((60, width, size), BF16),
-            pltpu.VMEM((2, 4, 2, width, size), F32),
-            pltpu.VMEM((nx, slice_rows + 8, width), F32),
-            pltpu.VMEM((nx, slice_rows + 8, width), F32),
-            pltpu.VMEM((RING, slice_rows // RING + 8, width), F32),
-            pltpu.VMEM((RING, slice_rows // RING + 8, width), F32),
-            pltpu.VMEM((RING, slice_rows // RING + 8, width), F32),
+            pltpu.VMEM((SCATTER_MAIL, size, width), BF16),
+            pltpu.VMEM((SCATTER_MAIL, size, width), BF16),
+            pltpu.VMEM((2, 4, 2, size, width), F32),
+            pltpu.VMEM((nx, slice_rows + EXTRA, width), F32),
+            pltpu.VMEM((nx, slice_rows + EXTRA, width), F32),
+            pltpu.VMEM((RING, slice_rows // RING + EXTRA, width), F32),
+            pltpu.VMEM((RING, slice_rows // RING + EXTRA, width), F32),
+            pltpu.VMEM((RING, slice_rows // RING + EXTRA, width), F32),
             pltpu.VMEM((RING, slice_rows // RING, width), F32),
             pltpu.SemaphoreType.DMA((BACK_MAIL,)),
             pltpu.SemaphoreType.DMA((BACK_MAIL,)),
         ],
         compiler_params=pltpu.CompilerParams(
-            collective_id=1, has_side_effects=True, vmem_limit_bytes=48 << 20
+            collective_id=1, has_side_effects=True, vmem_limit_bytes=24 << 20
         ),
         name="back_sums",
-    )(turned, wpart, bpart)
+    )(sums, wpart, bpart)
+
+
+def hand_over(*arrays):
+    def body(*refs):
+        for source, target in zip(refs[: len(arrays)], refs[len(arrays) :]):
+            target[...] = source[...]
+
+    vmem = pl.BlockSpec(memory_space=pltpu.VMEM)
+    return pl.pallas_call(
+        body,
+        out_shape=tuple(jax.ShapeDtypeStruct(a.shape, a.dtype) for a in arrays),
+        in_specs=[vmem] * len(arrays),
+        out_specs=(vmem,) * len(arrays),
+        compiler_params=pltpu.CompilerParams(vmem_limit_bytes=4 << 20),
+        name="hand_over",
+    )(*arrays)
 
 
 def local(features, adjacency, block_cols, block_live, weight, bias, upstream):
@@ -552,13 +609,13 @@
     piece, width = features.shape
     adj = adjacency.reshape(rows, slots, size, size)
     blocks = piece * lax.axis_size("row") // size
-    cols = block_cols.reshape(rows, slots).T
+    cols = block_cols.transpose(2, 1, 0)
     live = block_live.reshape(1, rows)
     act, grads, wpart, bpart = forward_layer(
         cols, live, features, adj, weight, bias.reshape(1, width), upstream
     )
-    turned = backward_product(cols, live, adj, grads.reshape(rows, size, width), blocks)
-    feature_grad, wgrad, bgrad = back_sums(turned, wpart, bpart, piece)
+    sums, act = backward_product(cols, live, adj, grads.reshape(rows, size, width), act, blocks)
+    feature_grad, wgrad, bgrad = hand_over(*back_sums(sums, wpart, bpart, piece))
     return act, feature_grad, wgrad, bgrad.reshape(width)
 
 

time: 139 us -> 108 us (0.78)
  Pallas kernels: 130 us -> 104 us
  local copies, waits for them, and re-layouts: 7.75 us -> 2.55 us
    pallas_call x1 -> x2, Pallas kernels: 27.7 us -> 11.7 us  [the longest x1 10.9 us: backward_product(): pl.pallas_call(backward_body, out_shape=(jax.ShapeDtypeStruct((blocks, si...]
    pallas_call x1, Pallas kernels: 66 us -> 60.8 us  [forward_layer(): pl.pallas_call(forward_body, out_shape=(jax.ShapeDtypeStruct((piece, widt...]
    unnamed x19 -> x12, local copies, waits for them, and re-layouts: 7.75 us -> 2.55 us
    pallas_call x1, Pallas kernels: 36 us -> 31.7 us  [back_sums(): pl.pallas_call(back_body, out_shape=(jax.ShapeDtypeStruct((piece, width),...]
where the time goes in v3:
time: 108 us
  Pallas kernels  104 us (96%)
  local copies, waits for them, and re-layouts  2.55 us (2%)
    pallas_call x1, Pallas kernels, forward_layer(): pl.pallas_call(forward_body, out_shape=(jax.ShapeDtypeStruct((piece, widt...  60.8 us
    pallas_call x1, Pallas kernels, back_sums(): pl.pallas_call(back_body, out_shape=(jax.ShapeDtypeStruct((piece, width),...  31.7 us
    pallas_call x1, Pallas kernels, backward_product(): pl.pallas_call(backward_body, out_shape=(jax.ShapeDtypeStruct((blocks, si...  10.9 us
    unnamed x12, local copies, waits for them, and re-layouts  2.55 us

profile of v3, /device:TPU:1, one launch (start us, length us, event | category | flops | bytes accessed | tf_op | source)
XLA Modules:
  0.0 107.6 jit_solution(12224013860988473210)
XLA Ops:
  0.6 0.0 copy-start.3
  0.6 0.0 copy-start.5
  0.7 60.8 %forward_layer.1 = (bf16[512,256]{1,0:T(8,128)(2,1)}, bf16[8,512,256]{2,1,0:T(8,128)(2,1)}, f32[256,256]{1,0:T(8,128)}, f32[8,256]{1,0:T(8,128)}) custom-call(s32[12,1,32]{2,1,0:T(1,128)} %bitcast.7, s32[1,32]{1,0:T(1,128)} %bitcast.9, bf16[512,256]{1,0:T(8,128)(2,1)} %features_ref.1, bf16[32,12,128,128]{3,2,1,0:T(8,128)(2,1)} %bitcast.11, ...), custom_call_target="tpu_custom_call" | custom-call | tf_op jit(solution)/shard_map/forward_layer/pallas_call | solution.py:293
  61.5 0.0 copy-done.3
  61.5 0.0 copy-done.5
  61.5 0.0 copy-start
  61.5 1.6 %copy-done = bf16[8,512,256]{2,1,0:T(8,128)(2,1)S(1)} copy-done((bf16[8,512,256]{2,1,0:T(8,128)(2,1)S(1)}, bf16[8,512,256]{2,1,0:T(8,128)(2,1)}, u32[]{:S(2)}) %copy-start) | copy-done | bytes 2097176
  63.1 0.0 copy-start.1
  63.1 0.9 copy-done.1
  64.1 0.0 copy-start.2
  64.1 0.0 copy-start.4
  64.1 10.9 %backward_product.1 = (bf16[64,128,256]{2,1,0:T(8,128)(2,1)S(1)}, bf16[512,256]{1,0:T(8,128)(2,1)}) custom-call(s32[12,1,32]{2,1,0:T(1,128)S(1)} %bitcast.8, s32[1,32]{1,0:T(1,128)S(1)} %bitcast.10, bf16[32,12,128,128]{3,2,1,0:T(8,128)(2,1)} %bitcast.12, bf16[32,128,256]{2,1,0:T(8,128)(2,1)S(1)} %bitcast.6, bf16[512,256]{1,0:T(8,128)(2,1)S(1)} %copy-done.1), custom_call_target="tpu_custom_call" | custom-call | tf_op jit(solution)/shard_map/backward_product/pallas_call | solution.py:373
  75.0 0.0 copy-done.2
  75.0 0.0 copy-done.4
  75.0 31.7 %back_sums.1 = (bf16[512,256]{1,0:T(8,128)(2,1)S(1)}, f32[256,256]{1,0:T(8,128)S(1)}, f32[1,256]{1,0:T(1,128)S(1)}) custom-call(bf16[64,128,256]{2,1,0:T(8,128)(2,1)S(1)} %get-tuple-element.19.sums_ref, f32[256,256]{1,0:T(8,128)S(1)} %copy-done.2, f32[8,256]{1,0:T(8,128)S(1)} %copy-done.4), custom_call_target="tpu_custom_call" | custom-call | tf_op jit(solution)/shard_map/back_sums/pallas_call | solution.py:562
  106.7 0.8 hand_over.1
Async XLA Ops:
  0.6 60.9 %copy-start.3 = (s32[32,1,12]{0,1,2:T(1,128)S(1)}, s32[32,1,12]{0,1,2:T(1,128)}, u32[]{:S(2)}) copy-start(s32[32,1,12]{0,1,2:T(1,128)} %param.9) | copy-start | bytes 4612
  0.6 60.9 %copy-start.5 = (s32[32,1]{0,1:T(1,128)S(1)}, s32[32,1]{0,1:T(1,128)}, u32[]{:S(2)}) copy-start(s32[32,1]{0,1:T(1,128)} %param.10) | copy-start | bytes 388
  61.5 1.6 %copy-start = (bf16[8,512,256]{2,1,0:T(8,128)(2,1)S(1)}, bf16[8,512,256]{2,1,0:T(8,128)(2,1)}, u32[]{:S(2)}) copy-start(bf16[8,512,256]{2,1,0:T(8,128)(2,1)} %get-tuple-element.16) | copy-start | bytes 6291460
  63.1 0.9 copy-start.1
  64.1 10.9 %copy-start.2 = (f32[256,256]{1,0:T(8,128)S(1)}, f32[256,256]{1,0:T(8,128)}, u32[]{:S(2)}) copy-start(f32[256,256]{1,0:T(8,128)} %get-tuple-element.20.wpart_ref) | copy-start | bytes 786436
  64.1 10.9 %copy-start.4 = (f32[8,256]{1,0:T(8,128)S(1)}, f32[8,256]{1,0:T(8,128)}, u32[]{:S(2)}) copy-start(f32[8,256]{1,0:T(8,128)} %get-tuple-element.21.bpart_ref) | copy-start | bytes 24580

commit v4 on v3

--- a/solution.py
+++ b/solution.py
@@ -60,11 +60,15 @@
             copy.wait_send()
 
 
-def meet(peers):
+def greet(peers):
     barrier = pltpu.get_barrier_semaphore()
     for peer in peers:
         pl.semaphore_signal(barrier, inc=1, device_id=peer, device_id_type=MESH)
-    pl.semaphore_wait(barrier, len(peers))
+    return barrier, len(peers)
+
+
+def meet(peers):
+    pl.semaphore_wait(*greet(peers))
 
 
 OFFSETS = (0, -1, 1, 2)
@@ -75,6 +79,9 @@
 
 
 def gather_rows(mail, base, here, panel):
+    def view(at, count):
+        return panel.at[pl.ds(at, count)]
+
     def index(f, dp, dq):
         return here.rows(*flavour(f, dp, dq)) * 4 + 2 * f
 
@@ -85,7 +92,7 @@
         return here.plane(*(flavour(f, d, 0) if slot == 0 else flavour(f, 0, d)))
 
     def pair(f, slot, dp):
-        blocks = panel.at[pl.ds(index(f, dp, 0), 2)]
+        blocks = view(index(f, dp, 0), 2)
         mail.post(number(f, slot, 0), blocks, blocks, to(f, slot, 1))
         mail.post(number(f, slot, 1), blocks, blocks, to(f, slot, -1))
 
@@ -94,24 +101,21 @@
 
     def onward(f, slot):
         at = where(f, slot, -1)
-        mail.take(number(f, slot, 0), panel.at[pl.ds(at, 2)])
-        block = panel.at[pl.ds(at, 1)]
-        mail.post(number(f, slot, 2), block, block, to(f, slot, 1))
+        mail.take(number(f, slot, 0), view(at, 2))
+        mail.post(number(f, slot, 2), view(at, 1), view(at, 1), to(f, slot, 1))
         at = where(f, slot, 1)
-        mail.take(number(f, slot, 1), panel.at[pl.ds(at, 2)])
-        block = panel.at[pl.ds(at + 1, 1)]
-        mail.post(number(f, slot, 3), block, block, to(f, slot, -1))
+        mail.take(number(f, slot, 1), view(at, 2))
+        mail.post(number(f, slot, 3), view(at + 1, 1), view(at + 1, 1), to(f, slot, -1))
 
     def last(f, slot):
         at = where(f, slot, 2)
-        mail.take(number(f, slot, 2), panel.at[pl.ds(at, 1)])
-        mail.take(number(f, slot, 3), panel.at[pl.ds(at + 1, 1)])
+        mail.take(number(f, slot, 2), view(at, 1))
+        mail.take(number(f, slot, 3), view(at + 1, 1))
 
     both = (0, 1)
-    for f in both:
-        pair(f, 0, 0)
-    for f in both:
-        pair(f, 1, 0)
+    for slot in (0, 1):
+        for f in both:
+            pair(f, slot, 0)
     for f in both:
         onward(f, 0)
         pair(f, 2, -1)
@@ -135,46 +139,47 @@
 
 
 def forward_body(
-    cols_ref, live_ref, features_ref, adj_hbm, weight_ref, bias_ref, upstream_ref,
+    cols_ref, live_ref, features_hbm, adj_hbm, weight_hbm, bias_hbm, upstream_hbm,
     act_ref, grad_hbm, wpart_ref, bpart_ref,
-    panel, adj, cross_out, cross_in, own, line_out, line_in, grads,
-    sent, came, adj_sem, out_sem,
+    panel, adj, weight, bias, upstream, cross_out, cross_in, own, line_out, line_in, grads,
+    sent, came, adj_sem, out_sem, in_sem,
 ):
     here = Place()
     mail = Mail(here, sent, came)
     rows, slots, size, _ = adj.shape
-    width = features_ref.shape[1]
+    per, _, width = features_hbm.shape
     blocks = panel.shape[0] - 1
-    piece = features_ref.shape[0]
-    half = piece // 2
-    per = piece // size
+    piece = per * size
     parts = adj_sem.shape[0]
     step = rows // parts
-    fetch = [
+    mine = pltpu.make_async_copy(features_hbm, panel.at[pl.ds(here.row * per, per)], in_sem.at[0])
+    later = [
+        pltpu.make_async_copy(source, target, in_sem.at[1 + n])
+        for n, (source, target) in enumerate(((weight_hbm, weight), (bias_hbm, bias), (upstream_hbm, upstream)))
+    ]
+    later += [
         pltpu.make_async_copy(adj_hbm.at[pl.ds(n * step, step)], adj.at[pl.ds(n * step, step)], adj_sem.at[n])
         for n in range(parts)
     ]
-    meet([here.plane(0, 1), here.plane(0, -1), here.plane(1, 0), here.plane(-1, 0),
-          here.line(1), here.line(-1), here.line(0, 1)])
-    for b in range(per):
-        panel[here.row * per + b] = features_ref[pl.ds(b * size, size), :]
+    barrier = greet([here.plane(0, 1), here.plane(0, -1), here.plane(1, 0), here.plane(-1, 0),
+                     here.line(1), here.line(-1), here.line(0, 1)])
+    for copy in [mine] + later:
+        copy.start()
     panel[blocks] = jnp.zeros_like(panel[blocks])
-    for copy in fetch:
-        copy.start()
+    mine.wait()
+    pl.semaphore_wait(*barrier)
     gather_rows(mail, 0, here, panel)
-    for copy in fetch:
+    for copy in later:
         copy.wait()
 
+    half = piece // 2
+
     def row_product(i):
-        total = None
-        for k in range(0, slots, 2):
-            left = jnp.concatenate([adj[i, k], adj[i, k + 1]], axis=1)
-            right = jnp.concatenate(
-                [panel[jnp.where(s < live_ref[0, i], cols_ref[s, 0, i], blocks)] for s in (k, k + 1)], axis=0
-            )
-            part = dot(left, right)
-            total = part if total is None else total + part
-        return total
+        left = jnp.concatenate([adj[i, k] for k in range(slots)], axis=1)
+        right = jnp.concatenate(
+            [panel[jnp.where(k < live_ref[0, i], cols_ref[k, 0, i], blocks)] for k in range(slots)], axis=0
+        )
+        return dot(left, right)
 
     def piece_product(dest, out):
         for n in range(per):
@@ -199,16 +204,15 @@
     line = number + 4
     up, down = here.line(1), here.line(-1)
     cross(0)
-    cross(1)
     keep(0)
     line_out[0] = chip(0, pl.ds(0, piece)).astype(BF16)
     mail.post(line, line_out.at[0, low], line_in.at[0], up)
     mail.post(line + 1, line_out.at[0, high], line_in.at[1], down)
-    cross(2)
+    cross(1)
     keep(1)
     line_out[1, high, :] = chip(1, high).astype(BF16)
     mail.post(line + 2, line_out.at[1, high], line_in.at[2], up)
-    cross(3)
+    cross(2)
     keep(2)
     line_out[2, low, :] = chip(2, low).astype(BF16)
     mail.post(line + 3, line_out.at[2, low], line_in.at[3], down)
@@ -218,6 +222,7 @@
     mail.take(line + 1, line_in.at[1])
     line_out[2, high, :] = (chip(2, high) + line_in[1].astype(F32)).astype(BF16)
     mail.post(line + 5, line_out.at[2, high], line_in.at[5], down)
+    cross(3)
     keep(3)
 
     ring = line + 6
@@ -230,12 +235,12 @@
         mail.take(line + a, line_in.at[a])
         mail.take(line + b, line_in.at[b])
         aggregated = (chip(3, at) + line_in[a].astype(F32) + line_in[b].astype(F32)).astype(BF16)
-        preact = dot(aggregated, weight_ref[...]) + bias_ref[...]
+        preact = dot(aggregated, weight[...]) + bias[...]
         s = jax.nn.sigmoid(preact)
         act_ref[at, :] = (preact * s).astype(BF16)
         derivative = s * (1.0 + preact * (1.0 - s))
-        grad_pre = (upstream_ref[at, :].astype(F32) * derivative).astype(BF16)
-        grads[mine, at, :] = dot(grad_pre, weight_ref[...], ((1,), (1,))).astype(BF16)
+        grad_pre = (upstream[at, :].astype(F32) * derivative).astype(BF16)
+        grads[mine, at, :] = dot(grad_pre, weight[...], ((1,), (1,))).astype(BF16)
         block = grads.at[mine, at]
         mail.post(ring + 2 * part, block, block, up)
         mail.post(ring + 2 * part + 1, block, block, down)
@@ -285,7 +290,8 @@
 
 def forward_layer(cols, live, features, adj, weight, bias, upstream):
     rows, slots, size, _ = adj.shape
-    piece, width = features.shape
+    per, _, width = features.shape
+    piece = per * size
     blocks = lax.axis_size("row") * piece // size
     pieces = lax.axis_size("col")
     vmem, anywhere = pl.BlockSpec(memory_space=pltpu.VMEM), pl.BlockSpec(memory_space=pl.ANY)
@@ -294,15 +300,18 @@
         forward_body,
         out_shape=(
             jax.ShapeDtypeStruct((piece, width), BF16),
-            jax.ShapeDtypeStruct((pieces, piece, width), BF16),
+            jax.ShapeDtypeStruct((SPACE * pieces, piece, width), BF16),
             jax.ShapeDtypeStruct((width, width), F32),
             jax.ShapeDtypeStruct((8, width), F32),
         ),
-        in_specs=[smem, smem, vmem, anywhere, vmem, vmem, vmem],
+        in_specs=[smem, smem] + [anywhere] * 5,
         out_specs=(vmem, anywhere, vmem, vmem),
         scratch_shapes=[
             pltpu.VMEM((blocks + 1, size, width), BF16),
             pltpu.VMEM(adj.shape, BF16),
+            pltpu.VMEM(weight.shape, BF16),
+            pltpu.VMEM(bias.shape, F32),
+            pltpu.VMEM(upstream.shape, BF16),
             pltpu.VMEM((4, piece, width), BF16),
             pltpu.VMEM((4, piece, width), BF16),
             pltpu.VMEM((4, piece, width), F32),
@@ -313,6 +322,7 @@
             pltpu.SemaphoreType.DMA((FORWARD_MAIL,)),
             pltpu.SemaphoreType.DMA((4,)),
             pltpu.SemaphoreType.DMA((8,)),
+            pltpu.SemaphoreType.DMA((4,)),
         ],
         compiler_params=pltpu.CompilerParams(
             collective_id=0, has_side_effects=True, vmem_limit_bytes=56 << 20
@@ -322,10 +332,11 @@
 
 
 PARTS = 4
+SPACE = 16
 
 
 def backward_body(
-    cols_ref, live_ref, adj_hbm, grad_hbm, act_hbm, out, act_out_hbm, adj, grad, acc, in_sem, act_sem
+    cols_ref, live_ref, adj_hbm, grad_hbm, out, adj, grad, acc, in_sem
 ):
     rows, slots, size, _ = adj.shape
     blocks = out.shape[0]
@@ -341,8 +352,6 @@
     for n in range(PARTS):
         for copy in fetch(n):
             copy.start()
-    passing = pltpu.make_async_copy(act_hbm, act_out_hbm, act_sem)
-    passing.start()
 
     @pl.loop(0, blocks)
     def _(j):
@@ -363,31 +372,25 @@
         for u in range(group):
             out[n * group + u] = acc[n * group + u].astype(out.dtype)
 
-    passing.wait()
-
-
-def backward_product(cols, live, adj, grad, act, blocks):
+
+def backward_product(cols, live, adj, grad, blocks):
     rows, slots, size, _ = adj.shape
     width = grad.shape[2]
     vmem, smem, anywhere = pl.BlockSpec(memory_space=pltpu.VMEM), pl.BlockSpec(memory_space=pltpu.SMEM), pl.BlockSpec(memory_space=pl.ANY)
     return pl.pallas_call(
         backward_body,
-        out_shape=(
-            jax.ShapeDtypeStruct((blocks, size, width), BF16),
-            jax.ShapeDtypeStruct(act.shape, BF16),
-        ),
-        in_specs=[smem, smem, anywhere, anywhere, anywhere],
-        out_specs=(vmem, anywhere),
+        out_shape=jax.ShapeDtypeStruct((blocks, size, width), BF16),
+        in_specs=[smem, smem, anywhere, anywhere],
+        out_specs=vmem,
         scratch_shapes=[
             pltpu.VMEM(adj.shape, BF16),
-            pltpu.VMEM(grad.shape, BF16),
+            pltpu.VMEM((rows, size, width), BF16),
             pltpu.VMEM((blocks + 1, size, width), F32),
             pltpu.SemaphoreType.DMA((2, PARTS)),
-            pltpu.SemaphoreType.DMA,
         ],
         compiler_params=pltpu.CompilerParams(vmem_limit_bytes=40 << 20),
         name="backward_product",
-    )(cols, live, adj, grad, act)
+    )(cols, live, adj, grad)
 
 
 SCATTER_MAIL = 60
@@ -612,10 +615,10 @@
     cols = block_cols.transpose(2, 1, 0)
     live = block_live.reshape(1, rows)
     act, grads, wpart, bpart = forward_layer(
-        cols, live, features, adj, weight, bias.reshape(1, width), upstream
+        cols, live, features.reshape(piece // size, size, width), adj, weight, bias.reshape(1, width), upstream
     )
-    sums, act = backward_product(cols, live, adj, grads.reshape(rows, size, width), act, blocks)
-    feature_grad, wgrad, bgrad = hand_over(*back_sums(sums, wpart, bpart, piece))
+    sums = backward_product(cols, live, adj, grads.reshape(SPACE * rows, size, width), blocks)
+    act, feature_grad, wgrad, bgrad = hand_over(act, *back_sums(sums, wpart, bpart, piece))
     return act, feature_grad, wgrad, bgrad.reshape(width)
 
 

time: 108 us -> 104 us (0.963)
  local copies, waits for them, and re-layouts: 2.55 us -> 0.02 us
    unnamed x12 -> x10, local copies, waits for them, and re-layouts: 2.55 us -> 0.02 us
where the time goes in v4:
time: 104 us
  Pallas kernels  103 us (99%)
    pallas_call x1, Pallas kernels, forward_layer(): pl.pallas_call(forward_body, out_shape=(jax.ShapeDtypeStruct((piece, widt...  60.5 us
    pallas_call x1, Pallas kernels, back_sums(): pl.pallas_call(back_body, out_shape=(jax.ShapeDtypeStruct((piece, width),...  31.1 us
    pallas_call x1, Pallas kernels, backward_product(): pl.pallas_call(backward_body, out_shape=jax.ShapeDtypeStruct((blocks, siz...  10.9 us

profile of v4, /device:TPU:1, one launch (start us, length us, event | category | flops | bytes accessed | tf_op | source)
XLA Modules:
  0.0 104.2 jit_solution(14214720583319587242)
XLA Ops:
  0.6 0.0 copy-start.4
  0.6 0.0 copy-start.2
  0.7 60.5 %forward_layer.1 = (bf16[512,256]{1,0:T(8,128)(2,1)}, bf16[128,512,256]{2,1,0:T(8,128)(2,1)}, f32[256,256]{1,0:T(8,128)}, f32[8,256]{1,0:T(8,128)}) custom-call(s32[12,1,32]{2,1,0:T(1,128)} %bitcast.7, s32[1,32]{1,0:T(1,128)} %bitcast.9, bf16[4,128,256]{2,1,0:T(8,128)(2,1)} %bitcast.14, bf16[32,12,128,128]{3,2,1,0:T(8,128)(2,1)} %bitcast.11, ...), custom_call_target="tpu_custom_call" | custom-call | tf_op jit(solution)/shard_map/forward_layer/pallas_call | solution.py:299
  61.2 0.0 copy-done.4
  61.2 0.0 copy-done.2
  61.2 0.0 copy-start
  61.2 0.0 copy-start.3
  61.2 0.0 copy-start.1
  61.2 10.9 %backward_product.1.sums_ref = bf16[64,128,256]{2,1,0:T(8,128)(2,1)S(1)} custom-call(s32[12,1,32]{2,1,0:T(1,128)S(1)} %bitcast.8, s32[1,32]{1,0:T(1,128)S(1)} %bitcast.10, bf16[32,12,128,128]{3,2,1,0:T(8,128)(2,1)} %bitcast.12, bf16[512,128,256]{2,1,0:T(8,128)(2,1)} %bitcast.13), custom_call_target="tpu_custom_call" | custom-call | tf_op jit(solution)/shard_map/backward_product/pallas_call | solution.py:380
  72.1 0.0 copy-done
  72.2 0.0 copy-done.3
  72.2 31.1 %back_sums.1 = (bf16[512,256]{1,0:T(8,128)(2,1)S(1)}, f32[256,256]{1,0:T(8,128)S(1)}, f32[1,256]{1,0:T(1,128)S(1)}) custom-call(bf16[64,128,256]{2,1,0:T(8,128)(2,1)S(1)} %backward_product.1.sums_ref, f32[256,256]{1,0:T(8,128)S(1)} %copy-done, f32[8,256]{1,0:T(8,128)S(1)} %copy-done.3), custom_call_target="tpu_custom_call" | custom-call | tf_op jit(solution)/shard_map/back_sums/pallas_call | solution.py:565
  103.2 0.0 copy-done.1
  103.2 0.9 hand_over.1
Async XLA Ops:
  0.6 60.5 %copy-start.4 = (s32[32,1]{0,1:T(1,128)S(1)}, s32[32,1]{0,1:T(1,128)}, u32[]{:S(2)}) copy-start(s32[32,1]{0,1:T(1,128)} %param.10) | copy-start | bytes 388
  0.6 60.5 %copy-start.2 = (s32[32,1,12]{0,1,2:T(1,128)S(1)}, s32[32,1,12]{0,1,2:T(1,128)}, u32[]{:S(2)}) copy-start(s32[32,1,12]{0,1,2:T(1,128)} %param.9) | copy-start | bytes 4612
  61.2 11.0 %copy-start = (f32[256,256]{1,0:T(8,128)S(1)}, f32[256,256]{1,0:T(8,128)}, u32[]{:S(2)}) copy-start(f32[256,256]{1,0:T(8,128)} %get-tuple-element.17.wpart_ref) | copy-start | bytes 786436
  61.2 11.0 %copy-start.3 = (f32[8,256]{1,0:T(8,128)S(1)}, f32[8,256]{1,0:T(8,128)}, u32[]{:S(2)}) copy-start(f32[8,256]{1,0:T(8,128)} %get-tuple-element.18.bpart_ref) | copy-start | bytes 24580
  61.2 42.0 %copy-start.1 = (bf16[512,256]{1,0:T(8,128)(2,1)S(1)}, bf16[512,256]{1,0:T(8,128)(2,1)}, u32[]{:S(2)}) copy-start(bf16[512,256]{1,0:T(8,128)(2,1)} %get-tuple-element.15.refs_0_) | copy-start | bytes 786436

commit v5 on v4

--- a/solution.py
+++ b/solution.py
@@ -65,10 +65,6 @@
     for peer in peers:
         pl.semaphore_signal(barrier, inc=1, device_id=peer, device_id_type=MESH)
     return barrier, len(peers)
-
-
-def meet(peers):
-    pl.semaphore_wait(*greet(peers))
 
 
 OFFSETS = (0, -1, 1, 2)
@@ -134,7 +130,7 @@
 
 
 GATHER_MAIL = 40
-FORWARD_MAIL = GATHER_MAIL + 4 + 6 + 6 + 5
+FORWARD_MAIL = GATHER_MAIL + 4 + 6 + 6 + 5 + 1
 EXTRA = 8
 
 
@@ -203,11 +199,22 @@
 
     line = number + 4
     up, down = here.line(1), here.line(-1)
-    cross(0)
-    keep(0)
-    line_out[0] = chip(0, pl.ds(0, piece)).astype(BF16)
-    mail.post(line, line_out.at[0, low], line_in.at[0], up)
-    mail.post(line + 1, line_out.at[0, high], line_in.at[1], down)
+    halves = (low, high)
+    spare = FORWARD_MAIL - 1
+
+    def half_product(dest, part, out):
+        for n in range(per // 2):
+            rows_at = part.start + n * size
+            out[rows_at : rows_at + size, :] = row_product(dest * per + rows_at // size).astype(out.dtype)
+
+    for part, at in zip(halves, (number, spare)):
+        half_product(here.cols(offsets[0], 1), part, cross_out.at[0])
+        mail.post(at, cross_out.at[0, part], cross_in.at[0, part], here.line(0, 1))
+    for n, (part, at, to) in enumerate(zip(halves, (number, spare), (up, down))):
+        half_product(here.cols(offsets[0]), part, own.at[0])
+        mail.take(at, cross_in.at[0, part])
+        line_out[0, part, :] = chip(0, part).astype(BF16)
+        mail.post(line + n, line_out.at[0, part], line_in.at[n], to)
     cross(1)
     keep(1)
     line_out[1, high, :] = chip(1, high).astype(BF16)
@@ -242,8 +249,13 @@
         grad_pre = (upstream[at, :].astype(F32) * derivative).astype(BF16)
         grads[mine, at, :] = dot(grad_pre, weight[...], ((1,), (1,))).astype(BF16)
         block = grads.at[mine, at]
-        mail.post(ring + 2 * part, block, block, up)
-        mail.post(ring + 2 * part + 1, block, block, down)
+        if part == 0:
+            mail.post(ring, block, block, up)
+        else:
+            mail.post(ring + 3, block, block, down)
+            mail.post(ring + 2, block, block, up)
+            block = grads.at[mine, low]
+            mail.post(ring + 1, block, block, down)
         w = dot(aggregated, grad_pre, ((0,), (0,)))
         b8 = jnp.sum(grad_pre.astype(F32).reshape(half // 8, 8, width), axis=0)
         wpart = w if wpart is None else wpart + w
@@ -262,10 +274,10 @@
     mail.take(ring, grads.at[before, low])
     block = grads.at[before, low]
     mail.post(ring + 4, block, block, up)
-    mail.take(ring + 1, grads.at[after, low])
     mail.take(ring + 3, grads.at[after, high])
     block = grads.at[after, high]
     mail.post(ring + 5, block, block, down)
+    mail.take(ring + 1, grads.at[after, low])
     mail.post(across + 1, grads.at[after], grads.at[after], here.line(0, 1))
     copies.append(out(after, 1))
     mail.take(ring + 2, grads.at[before, high])
@@ -336,11 +348,11 @@
 
 
 def backward_body(
-    cols_ref, live_ref, adj_hbm, grad_hbm, out, adj, grad, acc, in_sem
+    cols_ref, live_ref, adj_hbm, grad_hbm, acc, adj, grad, in_sem
 ):
     rows, slots, size, _ = adj.shape
-    blocks = out.shape[0]
-    step, group = rows // PARTS, blocks // PARTS
+    blocks = acc.shape[0] - 1
+    step = rows // PARTS
 
     def fetch(n):
         at = pl.ds(n * step, step)
@@ -367,11 +379,6 @@
                 j = jnp.where(k < live_ref[0, i], cols_ref[k, 0, i], blocks)
                 acc[j] += dot(adj[i, k], grad[i], ((0,), (0,)))
 
-    @pl.loop(0, PARTS)
-    def _(n):
-        for u in range(group):
-            out[n * group + u] = acc[n * group + u].astype(out.dtype)
-
 
 def backward_product(cols, live, adj, grad, blocks):
     rows, slots, size, _ = adj.shape
@@ -379,13 +386,12 @@
     vmem, smem, anywhere = pl.BlockSpec(memory_space=pltpu.VMEM), pl.BlockSpec(memory_space=pltpu.SMEM), pl.BlockSpec(memory_space=pl.ANY)
     return pl.pallas_call(
         backward_body,
-        out_shape=jax.ShapeDtypeStruct((blocks, size, width), BF16),
+        out_shape=jax.ShapeDtypeStruct((blocks + 1, size, width), F32),
         in_specs=[smem, smem, anywhere, anywhere],
         out_specs=vmem,
         scratch_shapes=[
             pltpu.VMEM(adj.shape, BF16),
             pltpu.VMEM((rows, size, width), BF16),
-            pltpu.VMEM((blocks + 1, size, width), F32),
             pltpu.SemaphoreType.DMA((2, PARTS)),
         ],
         compiler_params=pltpu.CompilerParams(vmem_limit_bytes=40 << 20),
@@ -410,13 +416,14 @@
     thin = slice_rows // RING
     peers = [here.plane(*at) for at in ((0, 1), (0, -1), (0, 2), (1, 0), (-1, 0), (2, 0))]
     peers += [(here.row, (here.col + d) % nx) for d in range(1, nx)]
+    barrier = greet(peers)
     for d in range(1, nx):
         c = (here.col + d) % nx
         w_out[c, :slice_rows] = wpart_ref[pl.ds(c * slice_rows, slice_rows), :]
         w_out[c, slice_rows:] = bpart_ref[...]
     w_in[here.col, :slice_rows] = wpart_ref[pl.ds(here.col * slice_rows, slice_rows), :]
     w_in[here.col, slice_rows:] = bpart_ref[...]
-    meet(peers)
+    pl.semaphore_wait(*barrier)
     base = SCATTER_MAIL
     for d in range(1, nx):
         c = (here.col + d) % nx
@@ -435,11 +442,8 @@
 
     def send(f, slot, kind, d, b):
         n = number(f, slot, kind)
-        if slot < 4:
-            src = source(f, slot, 2 if kind < 2 else d, b)
-        else:
-            src = tx.at[n]
-            tx[n] = source(f, slot, 2 if kind < 2 else d, b)[...].astype(BF16)
+        src = tx.at[n]
+        tx[n] = source(f, slot, 2 if kind < 2 else d, b)[...].astype(BF16)
         mail.post(n, src, rx.at[n], to(f, slot, d))
 
     def first(f, slot):

time: 104 us -> 103 us (level)
    pallas_call x1, Pallas kernels: 31.1 us -> 29.4 us  [back_sums(): pl.pallas_call(back_body, out_shape=(jax.ShapeDtypeStruct((piece, width),...]
where the time goes in v5:
time: 103 us
  Pallas kernels  102 us (99%)
    pallas_call x1, Pallas kernels, forward_layer(): pl.pallas_call(forward_body, out_shape=(jax.ShapeDtypeStruct((piece, widt...  60.8 us
    pallas_call x1, Pallas kernels, back_sums(): pl.pallas_call(back_body, out_shape=(jax.ShapeDtypeStruct((piece, width),...  29.4 us
    pallas_call x1, Pallas kernels, backward_product(): pl.pallas_call(backward_body, out_shape=jax.ShapeDtypeStruct((blocks + 1,...  10.9 us

profile of v5, /device:TPU:1, one launch (start us, length us, event | category | flops | bytes accessed | tf_op | source)
XLA Modules:
  0.0 102.8 jit_solution(17194972898197570679)
XLA Ops:
  0.6 0.0 copy-start.4
  0.6 0.0 copy-start.2
  0.7 60.8 %forward_layer.1 = (bf16[512,256]{1,0:T(8,128)(2,1)}, bf16[128,512,256]{2,1,0:T(8,128)(2,1)}, f32[256,256]{1,0:T(8,128)}, f32[8,256]{1,0:T(8,128)}) custom-call(s32[12,1,32]{2,1,0:T(1,128)} %bitcast.7, s32[1,32]{1,0:T(1,128)} %bitcast.9, bf16[4,128,256]{2,1,0:T(8,128)(2,1)} %bitcast.14, bf16[32,12,128,128]{3,2,1,0:T(8,128)(2,1)} %bitcast.11, ...), custom_call_target="tpu_custom_call" | custom-call | tf_op jit(solution)/shard_map/forward_layer/pallas_call | solution.py:311
  61.5 0.0 copy-done.4
  61.5 0.0 copy-done.2
  61.5 0.0 copy-start
  61.5 0.0 copy-start.3
  61.5 0.0 copy-start.1
  61.5 10.9 %backward_product.1.sums_ref = f32[65,128,256]{2,1,0:T(8,128)S(1)} custom-call(s32[12,1,32]{2,1,0:T(1,128)S(1)} %bitcast.8, s32[1,32]{1,0:T(1,128)S(1)} %bitcast.10, bf16[32,12,128,128]{3,2,1,0:T(8,128)(2,1)} %bitcast.12, bf16[512,128,256]{2,1,0:T(8,128)(2,1)} %bitcast.13), custom_call_target="tpu_custom_call" | custom-call | tf_op jit(solution)/shard_map/backward_product/pallas_call | solution.py:387
  72.5 0.0 copy-done
  72.5 0.0 copy-done.3
  72.5 29.4 %back_sums.1 = (bf16[512,256]{1,0:T(8,128)(2,1)S(1)}, f32[256,256]{1,0:T(8,128)S(1)}, f32[1,256]{1,0:T(1,128)S(1)}) custom-call(f32[65,128,256]{2,1,0:T(8,128)S(1)} %backward_product.1.sums_ref, f32[256,256]{1,0:T(8,128)S(1)} %copy-done, f32[8,256]{1,0:T(8,128)S(1)} %copy-done.3), custom_call_target="tpu_custom_call" | custom-call | tf_op jit(solution)/shard_map/back_sums/pallas_call | solution.py:569
  101.9 0.0 copy-done.1
  101.9 0.9 hand_over.1
Async XLA Ops:
  0.6 60.9 %copy-start.4 = (s32[32,1]{0,1:T(1,128)S(1)}, s32[32,1]{0,1:T(1,128)}, u32[]{:S(2)}) copy-start(s32[32,1]{0,1:T(1,128)} %param.10) | copy-start | bytes 388
  0.6 60.9 %copy-start.2 = (s32[32,1,12]{0,1,2:T(1,128)S(1)}, s32[32,1,12]{0,1,2:T(1,128)}, u32[]{:S(2)}) copy-start(s32[32,1,12]{0,1,2:T(1,128)} %param.9) | copy-start | bytes 4612
  61.5 10.9 %copy-start = (f32[256,256]{1,0:T(8,128)S(1)}, f32[256,256]{1,0:T(8,128)}, u32[]{:S(2)}) copy-start(f32[256,256]{1,0:T(8,128)} %get-tuple-element.17.wpart_ref) | copy-start | bytes 786436
  61.5 10.9 %copy-start.3 = (f32[8,256]{1,0:T(8,128)S(1)}, f32[8,256]{1,0:T(8,128)}, u32[]{:S(2)}) copy-start(f32[8,256]{1,0:T(8,128)} %get-tuple-element.18.bpart_ref) | copy-start | bytes 24580
  61.5 40.3 %copy-start.1 = (bf16[512,256]{1,0:T(8,128)(2,1)S(1)}, bf16[512,256]{1,0:T(8,128)(2,1)}, u32[]{:S(2)}) copy-start(bf16[512,256]{1,0:T(8,128)(2,1)} %get-tuple-element.15.refs_0_) | copy-start | bytes 786436
